TPU v7x, 512 devices: a whole 4x4x16 slice. The times are simulated.
512 devices in a mesh: snap: 16 (over y, x), plane: 32 (over z, core).
Axes of the slice: x: 4, y: 4, z: 16, core: 2. Of those that a mesh axis runs over, the one named last changes fastest.
Arguments:
- velocity: bfloat16 [16, 128, 3, 128, 128], P('snap', 'plane'), may hold values from -6 to 6
- plane_count: int32 [32], P('plane'), may hold values from 1 to 4, as said below
- inv_span: float32 [32, 4], P('plane'), may hold values from 0.5 to 4
- kernels: float32 [3, 2, 3, 3], replicated, may hold values from -2.4 to 2.4
- omega_block: int32 [32, 4], P('plane'), may hold values from 0 to 7
- omega_table: bfloat16 [8, 9, 32, 256], replicated, may hold values from -0.0625 to 0.0625
- omega_stream: bfloat16 [32, 256], replicated, may hold values from -6 to 6
- wall_shear: bfloat16 [16, 2, 128, 128], P('snap', None, 'plane'), may hold values from -6 to 6
Outputs:
- sketch: float32 [2, 32, 32, 256], P(None, 'plane', 'snap')
- gram: float32 [256, 256], replicated
Inputs may be any that keep to these rules, and one draw needn't show every extreme that they name: `plane_count`: every index of plane holds 1 or more live slots, slots 0 onwards; some index holds 4.
All inputs are finite; a program needn't handle non-finite values.
Results may differ from a plain program's by a relative error of at most 0.0043.
Values may be sent and summed in bfloat16 or wider, within the bound.
No kernel may reach another device: no remote copies, remote signals or barrier semaphores. Data moves between devices by JAX's collectives and lax.ppermute only.
A program may use at most 64 MiB of HBM per device.

v0:
```python
import jax
import jax.numpy as jnp
from jax import lax
from jax.sharding import PartitionSpec as P

X = 128
ZW = 128


def shifted(value, axis, steps):
    count = lax.axis_size(axis)
    leading, last = (max(0, -steps), min(count, count - steps))
    return lax.ppermute(value, axis, [(source, source + steps) for source in range(leading, last)])


def in_plane(centre, kernels):
    snaps, comps, zw, xw = centre.shape
    field = centre.astype(jnp.float32)
    padded = jnp.pad(field, ((0, 0), (0, 0), (1, 1), (1, 1)))
    first = jnp.zeros_like(field)
    second = jnp.zeros_like(field)
    for row_a in range(3):
        for col_b in range(3):
            window = padded[:, :, row_a : row_a + zw, col_b : col_b + xw]
            first = first + kernels[:, 0, row_a, col_b][None, :, None, None] * window
            second = second + kernels[:, 1, row_a, col_b][None, :, None, None] * window
    return (first, second)


def features(centre, below, above, span, kernels):
    snaps, comps, zw, xw = centre.shape
    first, second = in_plane(centre, kernels)
    normal = (above.astype(jnp.float32) - below.astype(jnp.float32)) * span
    grads = jnp.stack([first, second, normal], axis=2).reshape(snaps, 9, zw, xw)
    filtered = grads.reshape(snaps, 9, zw // 4, 4, xw // 4, 4).mean(axis=(3, 5))
    return filtered.astype(jnp.bfloat16)


def per_device(
    velocity, plane_count, inv_span, kernels, omega_block, omega_table, omega_stream, wall_shear
):
    slots = velocity.shape[1]
    live_count = plane_count[0]
    coef = jnp.zeros((velocity.shape[0], omega_stream.shape[1]), jnp.float32)
    last_live = lax.dynamic_index_in_dim(velocity, live_count - 1, 1, keepdims=False)
    from_below = shifted(last_live, "plane", 1)
    from_above = shifted(velocity[:, 0], "plane", -1)
    for slot in range(slots):
        below = from_below if slot == 0 else velocity[:, slot - 1]
        if slot + 1 < slots:
            above = jnp.where(slot + 1 < live_count, velocity[:, slot + 1], from_above)
        else:
            above = from_above
        feats = features(velocity[:, slot], below, above, inv_span[0, slot], kernels)
        proj = jnp.einsum("sczx,xk->sczk", feats, omega_stream, preferred_element_type=jnp.float32)
        table = lax.dynamic_index_in_dim(
            omega_table, omega_block[0, slot], 0, keepdims=False
        ).astype(jnp.float32)
        term = jnp.einsum("sczk,czk->sk", proj, table, precision=lax.Precision.HIGHEST)
        coef = coef + jnp.where(slot < live_count, term, jnp.zeros_like(term))
    coef = lax.psum(coef, "plane")
    snaps, comps, zw, xw = wall_shear.shape
    shear_f = (
        wall_shear.astype(jnp.float32)
        .reshape(snaps, comps, zw // 4, 4, xw // 4, 4)
        .mean(axis=(3, 5))
    )
    partial_sketch = jnp.einsum("smzx,sk->mzxk", shear_f, coef, precision=lax.Precision.HIGHEST)
    sketch = lax.psum_scatter(partial_sketch, "snap", scatter_dimension=2, tiled=True)
    total_rows = 2 * (X // 4) * (ZW // 4)
    flat = sketch.reshape(-1, sketch.shape[-1])
    local_gram = jnp.dot(flat.T, flat, precision=lax.Precision.HIGHEST)
    gram = lax.psum(local_gram, ("snap", "plane")) / jnp.float32(total_rows)
    return (sketch, gram)


def solution(mesh):
    return jax.shard_map(
        per_device,
        mesh=mesh,
        in_specs=(
            P("snap", "plane", None, None, None),
            P("plane"),
            P("plane", None),
            P(),
            P("plane", None),
            P(),
            P(),
            P("snap", None, "plane", None),
        ),
        out_specs=(P(None, "plane", "snap", None), P()),
        check_vma=False,
    )
```

profile of v0, /device:TPU:1, one launch (start us, length us, event | category | flops | bytes accessed | tf_op | source)
XLA Modules:
  0.0 789.9 jit_solution(1391584907513652331)
XLA Ops:
  7.2 0.0 copy-start
  7.2 0.0 copy-start.5
  7.2 0.0 copy-start.3
  7.2 0.0 copy-start.7
  7.2 0.0 all-reduce.10.cloned.1.call-start
  7.9 1.2 fusion.21
  9.1 8.7 %collective-permute-start = (bf16[1,3,128,128]{3,2,1,0:T(8,128)(2,1)S(1)}, bf16[1,3,128,128]{3,2,1,0:T(8,128)(2,1)S(1)}, u32[]{:S(2)}, u32[]{:S(2)}) collective-permute-start(bf16[1,3,128,128]{3,2,1,0:T(8,128)(2,1)S(1)} %get-tuple-element.29), channel_id=1, source_target_pairs={{1,0},{2,1},{3,2},{4,3},{5,4},{6,5},{7,6},{8,7},{9,8},{10,9},{11,1... | collective-permute-start | bytes 294920 | tf_op jit(solution)/shard_map/ppermute | solution.py:13
  17.8 1.9 collective-permute-start.1
  19.8 0.0 copy-done.5
  19.8 0.7 fusion.23
  25.5 0.0 copy-done.3
  25.6 0.2 slice_reduce_fusion.17
  25.8 0.1 reduce_sum.53
  25.9 0.1 reduce_sum.54
  28.6 1.3 add_bitcast_fusion.7
  29.9 0.0 copy-start.6
  29.9 0.0 copy-start.1
  29.9 1.3 add_bitcast_fusion.6
  31.3 0.7 fusion.22
  32.0 0.0 collective-permute-done
  32.0 0.0 collective-permute-done.1
  32.0 0.0 copy-done.1
  32.0 2.7 multiply_bitcast_fusion.3
  34.6 0.1 pad_maximum_fusion
  34.8 21.0 %reshape_reshape.12 = f32[9,32,4,32,4]{4,3,2,1,0:T(8,128)} reshape(f32[1,3,3,128,128]{4,3,2,1,0:T(8,128)S(1)} %copy.14) | data formatting | bytes 1179648 | tf_op jit(solution)/shard_map/reshape;reshape | solution.py:35
  55.8 7.9 %reduce_sum.55 = f32[9,32,32]{2,1,0:T(8,128)S(1)} reduce(f32[9,32,4,32,4]{4,3,2,1,0:T(8,128)} %reshape_reshape.12, f32[]{:T(128)} %constant.38.clone.1), dimensions={2,4}, to_apply=%region_2.3 | reduce | flops 138240 | bytes 626692 | tf_op jit(solution)/shard_map/reduce_sum | solution.py:35
  63.8 20.8 %reshape_reshape.13 = f32[9,32,4,32,4]{4,3,2,1,0:T(8,128)} reshape(f32[1,3,3,128,128]{4,3,2,1,0:T(8,128)S(1)} %copy.15) | data formatting | bytes 1179648 | tf_op jit(solution)/shard_map/reshape;reshape | solution.py:35
  84.6 7.9 %reduce_sum.56 = f32[9,32,32]{2,1,0:T(8,128)S(1)} reduce(f32[9,32,4,32,4]{4,3,2,1,0:T(8,128)} %reshape_reshape.13, f32[]{:T(128)} %constant.38.clone.1), dimensions={2,4}, to_apply=%region_3.4 | reduce | flops 138240 | bytes 626692 | tf_op jit(solution)/shard_map/reduce_sum | solution.py:35
  92.5 0.1 pad_maximum_fusion.2
  92.7 20.8 %reshape_reshape.14 = f32[9,32,4,32,4]{4,3,2,1,0:T(8,128)} reshape(f32[1,3,3,128,128]{4,3,2,1,0:T(8,128)S(1)} %copy.16) | data formatting | bytes 1179648 | tf_op jit(solution)/shard_map/reshape;reshape | solution.py:35
  113.5 7.9 %reduce_sum.57 = f32[9,32,32]{2,1,0:T(8,128)S(1)} reduce(f32[9,32,4,32,4]{4,3,2,1,0:T(8,128)} %reshape_reshape.14, f32[]{:T(128)} %constant.38.clone.1), dimensions={2,4}, to_apply=%region_4.5 | reduce | flops 138240 | bytes 626692 | tf_op jit(solution)/shard_map/reduce_sum | solution.py:35
  121.5 20.8 %reshape_reshape.15 = f32[9,32,4,32,4]{4,3,2,1,0:T(8,128)} reshape(f32[1,3,3,128,128]{4,3,2,1,0:T(8,128)S(1)} %copy.17) | data formatting | bytes 1179648 | tf_op jit(solution)/shard_map/reshape;reshape | solution.py:35
  142.4 8.0 %reduce_sum.58 = f32[9,32,32]{2,1,0:T(8,128)S(1)} reduce(f32[9,32,4,32,4]{4,3,2,1,0:T(8,128)} %reshape_reshape.15, f32[]{:T(128)} %constant.38.clone.1), dimensions={2,4}, to_apply=%region_5.6 | reduce | flops 138240 | bytes 626692 | tf_op jit(solution)/shard_map/reduce_sum | solution.py:35
  150.4 0.2 fusion.4
  150.6 0.2 fusion.5
  150.8 0.2 fusion.6
  151.0 0.2 fusion.7
  151.2 47.0 %psum.14 = f32[256]{0:T(256)S(1)} all-reduce(f32[256]{0:T(256)S(1)} %select_add_fusion), channel_id=1, replica_groups=mesh['snap'=16,'plane'=32] {'plane'}, use_global_device_ids=true, to_apply=%region_6.7 | all-reduce | flops 256 | bytes 2048 | tf_op jit(solution)/shard_map/psum | solution.py:61
  198.2 0.7 multiply_bitcast_fusion.4
  198.9 0.0 all-reduce.10.cloned.1.call-update
  198.9 0.0 all-reduce.8.cloned.1.call-start
  199.0 1.3 dynamic-slice
  200.9 109.3 %all-reduce.10.cloned.1.call-done = f32[2,1,32,256]{3,2,1,0:T(8,128)} async-done(((f32[2,1,32,256]{3,2,1,0:T(8,128)}), f32[2,1,32,256]{3,2,1,0:T(8,128)}) %all-reduce.10.cloned.1.call-update) | async-done | bytes 65552
  310.2 0.7 constant_dynamic-slice_fusion
  310.9 1.1 convolution_bitcast_fusion.4
  312.1 0.0 all-reduce.8.cloned.1.call-update
  312.1 469.3 %all-reduce.8.cloned.1.call-done = f32[256,256]{1,0:T(8,128)} async-done(((f32[256,256]{1,0:T(8,128)}), f32[256,256]{1,0:T(8,128)}) %all-reduce.8.cloned.1.call-update) | async-done | bytes 262160 | tf_op jit(solution)/shard_map/psum | solution.py:73
  781.4 1.7 broadcast_multiply_fusion
  (14 shorter events, 0.2 us)
Async XLA Ops:
  7.2 143.2 %copy-start = (bf16[32,256]{1,0:T(8,128)(2,1)S(1)}, bf16[32,256]{1,0:T(8,128)(2,1)}, u32[]{:S(2)}) copy-start(bf16[32,256]{1,0:T(8,128)(2,1)} %param.14) | copy-start | bytes 49156
  7.2 12.6 %copy-start.5 = (s32[1,4]{1,0:T(1,128)S(1)}, s32[1,4]{1,0:T(1,128)}, u32[]{:S(2)}) copy-start(s32[1,4]{1,0:T(1,128)} %param.12) | copy-start | bytes 52
  7.2 18.4 %copy-start.3 = (f32[3,2,3,3]{3,1,2,0:T(2,128)S(1)}, f32[3,2,3,3]{3,1,2,0:T(2,128)}, u32[]{:S(2)}) copy-start(f32[3,2,3,3]{3,1,2,0:T(2,128)} %param.11) | copy-start | bytes 652
  7.2 18.6 %copy-start.7 = (bf16[1,2,4,128]{3,2,1,0:T(4,128)(2,1)S(1)}, bf16[1,2,4,128]{3,2,1,0:T(4,128)(2,1)}, u32[]{:S(2)}) copy-start(bf16[1,2,4,128]{3,2,1,0:T(4,128)(2,1)} %param.15) | copy-start | bytes 6148
  7.2 303.0 %all-reduce.10.cloned.1.call-start = ((), (), s32[]{:S(2)}) async-start(), calls=%async_computation.1 | async-start | bytes 131072
  9.1 22.9 %collective-permute-start = (bf16[1,3,128,128]{3,2,1,0:T(8,128)(2,1)S(1)}, bf16[1,3,128,128]{3,2,1,0:T(8,128)(2,1)S(1)}, u32[]{:S(2)}, u32[]{:S(2)}) collective-permute-start(bf16[1,3,128,128]{3,2,1,0:T(8,128)(2,1)S(1)} %get-tuple-element.29), channel_id=1, source_target_pairs={{1,0},{2,1},{3,2},{4,3},{5,4},{6,5},{7,6},{8,7},{9,8},{10,9},{11,1... | collective-permute-start | bytes 294920 | tf_op jit(solution)/shard_map/ppermute | solution.py:13
  17.8 14.1 %collective-permute-start.1 = (bf16[1,3,128,128]{3,2,1,0:T(8,128)(2,1)S(1)}, bf16[1,3,128,128]{3,2,1,0:T(8,128)(2,1)S(1)}, u32[]{:S(2)}, u32[]{:S(2)}) collective-permute-start(bf16[1,3,128,128]{3,2,1,0:T(8,128)(2,1)S(1)} %get-tuple-element.28), channel_id=1, source_target_pairs={{0,1},{1,2},{2,3},{3,4},{4,5},{5,6},{6,7},{7,8},{8,9},{9,10},{10,1... | collective-permute-start | bytes 294920 | tf_op jit(solution)/shard_map/ppermute | solution.py:13
  29.9 1.4 copy-start.6
  29.9 2.0 copy-start.1
  142.3 8.0 %copy-start.2 = (bf16[8,9,32,256]{3,2,1,0:T(8,128)(2,1)S(1)}, bf16[8,9,32,256]{3,2,1,0:T(8,128)(2,1)}, u32[]{:S(2)}) copy-start(bf16[8,9,32,256]{3,2,1,0:T(8,128)(2,1)} %param.13) | copy-start | bytes 3538948
  198.9 582.5 %all-reduce.8.cloned.1.call-start = ((), (), s32[]{:S(2)}) async-start(), calls=%async_computation | async-start | bytes 524288 | tf_op jit(solution)/shard_map/psum | solution.py:73
  310.9 472.1 %copy-start.4 = (f32[2,1,2,256]{3,2,1,0:T(2,128)}, f32[2,1,2,256]{3,2,1,0:T(2,128)S(1)}, u32[]{:S(2)}) copy-start(f32[2,1,2,256]{3,2,1,0:T(2,128)S(1)} %constant_dynamic-slice_fusion) | copy-start | bytes 12292
Sparse Core Ops, SparseCore 0:
  199.0 111.1 all-reduce.9
  316.2 465.1 all-reduce.7
where the time goes:
time: 791 us; the launch traced here: 790 us
  waiting for transfers between devices  579 us (73%)
  local copies, waits for them, and re-layouts  87.4 us (11%)
  blocking collectives  47 us (6%)
  other arithmetic  40.9 us (5%)
  between operations  23.3 us (3%)
  starting transfers between devices  10.7 us (1%)
    psum x1, waiting for transfers between devices, per_device(): gram = lax.psum(local_gram, ('snap', 'plane')) / jnp.float32(total_rows)  469 us
    unnamed x3, waiting for transfers between devices  109 us
    another operation x4, local copies, waits for them, and re-layouts, features(): filtered = grads.reshape(snaps, 9, zw // 4, 4, xw // 4, 4).mean(axis=(3, 5))  83.6 us
    psum x1, blocking collectives, per_device(): coef = lax.psum(coef, 'plane')  47 us
    reduce_sum x4, other arithmetic, features(): filtered = grads.reshape(snaps, 9, zw // 4, 4, xw // 4, 4).mean(axis=(3, 5))  31.8 us
  transfers between devices with their start and end apart: 4, of which 2 were waited for; matrix products, arithmetic and copies ran while one was open for 1% of the time, Pallas kernels for 0%

commit v1 on v0

v1 whole, which is shorter than its diff:
```python
import jax
import jax.numpy as jnp
from jax import lax
from jax.experimental import pallas as pl
from jax.experimental.pallas import tpu as pltpu
from jax.sharding import Mesh, PartitionSpec as P

CAP = 4
ROWS = 1536
PAD = 8
SMALL = 1.0 / 16.0
HI = lax.Precision.HIGHEST


def iota(shape, dim):
    return lax.broadcasted_iota(jnp.int32, shape, dim)


def split(value):
    high = value.astype(jnp.bfloat16)
    low = (value - high.astype(jnp.float32)).astype(jnp.bfloat16)
    return high, low


def project_kernel(own, inner, outer, vel_hbm, table_hbm, stream, shear, out, vel, table, pooled, vsem, tsem):
    copies = []
    for c in range(CAP):
        part = pl.ds(c * 384, 384)
        copy = pltpu.make_async_copy(vel_hbm.at[part], vel.at[part], vsem.at[c])
        copy.start()
        copies.append(copy)
    table_copy = pltpu.make_async_copy(table_hbm, table, tsem)
    table_copy.start()

    count = own[8].astype(jnp.int32)
    odd = own[9] > 0.5
    far = own[10] > 0.5

    def pick(low, high):
        return jnp.where(odd, low, high)

    spans = [own[c] for c in range(CAP)]
    blocks = [own[4 + c].astype(jnp.int32) for c in range(CAP)]
    prev_last = jnp.maximum(pick(inner[8], outer[8]).astype(jnp.int32) - 1, 0)
    prev_span = pick(inner[prev_last], outer[prev_last])
    prev_block = pick(inner[4 + prev_last], outer[4 + prev_last]).astype(jnp.int32)
    next_span = pick(outer[0], inner[0])
    next_block = pick(outer[4], inner[4]).astype(jnp.int32)

    lane = iota((128, 128), 1)
    gap = iota((128, 128), 0) - 4 * (lane % 32) - lane // 32 + 1
    pool = jnp.where((gap >= 0) & (gap < 4) & (lane < 96), 1.0, 0.0).astype(jnp.bfloat16)

    group = iota((8, 128), 1) // 32

    def tap(i, q, a):
        at = 64 + ((i * 2 + q) * 3 + a) * 3
        picked = jnp.where(group == 0, own[at], jnp.where(group == 1, own[at + 1], own[at + 2]))
        return jnp.where(group < 3, picked * SMALL, 0.0)

    taps = {(i, q, a): tap(i, q, a) for i in range(3) for q in range(2) for a in range(3)}
    zeros = jnp.zeros((32, 256), jnp.bfloat16)
    omega = stream[...]
    spread = jnp.concatenate([omega, zeros, zeros, zeros], axis=0)
    centre = jnp.concatenate([zeros, omega, zeros, zeros] * 2, axis=0)
    first_row = iota((32, 128), 0) == 0
    last_row = iota((32, 128), 0) == 31

    planes, normals = [], []
    for c in range(CAP):
        copies[c].wait()
        pooled[pl.ds(PAD + c * 384, 384), :] = jnp.dot(
            vel[pl.ds(c * 384, 384), :], pool, preferred_element_type=jnp.float32
        )
    for c in range(CAP):
        feats, centres = [], []
        for i in range(3):
            base = PAD + (c * 3 + i) * 128
            row = [pooled[pl.ds(base + j, 32, stride=4), :] for j in range(4)]
            before = jnp.where(first_row, 0.0, pooled[pl.ds(base - 1, 32, stride=4), :])
            after = jnp.where(last_row, 0.0, pooled[pl.ds(base + 4, 32, stride=4), :])
            inside = row[1] + row[2]
            head = row[0] + inside
            window = (before + head, head + row[3], inside + row[3] + after)
            for q in range(2):
                mixed = sum(
                    (window[a].reshape(4, 8, 128) * taps[i, q, a][None]).reshape(32, 128) for a in range(3)
                )
                folded = mixed + pltpu.roll(mixed, 96, 1) + pltpu.roll(mixed, 64, 1)
                feats.append(folded.astype(jnp.bfloat16))
            centres.append(jnp.concatenate(split(window[1] * SMALL), axis=1))
        planes.append(
            jnp.dot(jnp.concatenate(feats, axis=0), spread, preferred_element_type=jnp.float32)
        )
        normals.append(
            jnp.dot(jnp.concatenate(centres, axis=0), centre, preferred_element_type=jnp.float32)
        )

    table_copy.wait()
    total = jnp.zeros((8, 256), jnp.float32)

    def rows_of(block, channel):
        return table[block, channel * 32 : channel * 32 + 32, :].astype(jnp.float32)

    for c in range(CAP):
        live = c < count
        alive = jnp.where(live, 1.0, 0.0)
        up_span = spans[c - 1] if c else prev_span
        up_block = blocks[c - 1] if c else prev_block
        if c + 1 < CAP:
            more = c + 1 < count
            down_span = jnp.where(more, spans[c + 1], next_span)
            down_block = jnp.where(more, blocks[c + 1], next_block)
        else:
            down_span, down_block = next_span, next_block
        part = jnp.zeros((8, 256), jnp.float32)
        for i in range(3):
            for q in range(2):
                at = (i * 2 + q) * 32
                part += (planes[c][at : at + 32] * rows_of(blocks[c], 3 * i + q)).reshape(4, 8, 256).sum(0)
            weight = up_span * rows_of(up_block, 3 * i + 2) - down_span * rows_of(down_block, 3 * i + 2)
            part += (normals[c][i * 32 : i * 32 + 32] * weight).reshape(4, 8, 256).sum(0)
        total += alive * part

    coef = jnp.sum(total, axis=0, keepdims=True)
    shear_pooled = jnp.dot(shear[...], pool, preferred_element_type=jnp.float32) * SMALL
    first = jnp.sum(shear_pooled[0:4], axis=0, keepdims=True)
    second = jnp.sum(shear_pooled[4:8], axis=0, keepdims=True)
    first = jnp.broadcast_to(first, (8, 128))
    second = jnp.broadcast_to(second, (8, 128))
    low = jnp.where(group == 0, pltpu.roll(first, 96, 1), jnp.where(group == 1, second, 0.0))
    wall = jnp.where(far, pltpu.roll(low, 64, 1), low)
    at_row = iota((8, 128), 0)
    tile = jnp.where(
        at_row == 0,
        jnp.broadcast_to(coef[:, :128], (8, 128)),
        jnp.where(at_row == 1, jnp.broadcast_to(coef[:, 128:], (8, 128)), jnp.where(at_row == 2, wall, 0.0)),
    )
    for copy_at in range(out.shape[0]):
        out[copy_at] = tile


def project(own, inner, outer, velocity, table, stream, shear, copies):
    smem = pl.BlockSpec(memory_space=pltpu.SMEM)
    vmem = pl.BlockSpec(memory_space=pltpu.VMEM)
    hbm = pl.BlockSpec(memory_space=pl.ANY)
    return pl.pallas_call(
        project_kernel,
        out_shape=jax.ShapeDtypeStruct((copies, 8, 128), jnp.float32),
        in_specs=[smem, smem, smem, hbm, hbm, vmem, vmem],
        out_specs=vmem,
        scratch_shapes=[
            pltpu.VMEM((ROWS, 128), jnp.bfloat16),
            pltpu.VMEM((8, 288, 256), jnp.bfloat16),
            pltpu.VMEM((ROWS + 2 * PAD, 128), jnp.float32),
            pltpu.SemaphoreType.DMA((CAP,)),
            pltpu.SemaphoreType.DMA,
        ],
        name="project",
    )(own, inner, outer, velocity, table, stream, shear)


def merge_kernel(rows, out):
    low = jnp.sum(rows[pl.ds(0, 16, stride=8), :], axis=0, keepdims=True)
    high = jnp.sum(rows[pl.ds(1, 16, stride=8), :], axis=0, keepdims=True)
    wall = rows[pl.ds(2, 8, stride=16), :] + rows[pl.ds(10, 8, stride=16), :]
    at_row = iota((8, 128), 0)
    coef = jnp.where(at_row == 0, low, jnp.where(at_row == 1, high, 0.0))
    tile = jnp.concatenate([wall, coef], axis=0)
    for copy_at in range(out.shape[0]):
        out[copy_at] = tile


def merge(rows, copies):
    return pl.pallas_call(
        merge_kernel,
        out_shape=jax.ShapeDtypeStruct((copies, 16, 128), jnp.float32),
        in_specs=[pl.BlockSpec(memory_space=pltpu.VMEM)],
        out_specs=pl.BlockSpec(memory_space=pltpu.VMEM),
        name="merge",
    )(rows)


def finish_kernel(place, rows, sketch, gram, full):
    def across(at):
        return rows[pl.ds(at, 16, stride=32), :]

    coef = jnp.concatenate([across(8) + across(24), across(9) + across(25)], axis=1)
    wall = jnp.concatenate([across(16 * core + r) for core in range(2) for r in range(8)], axis=1)
    inner = lax.dot_general(wall, wall, (((1,), (1,)), ((), ())), precision=HI, preferred_element_type=jnp.float32)
    right = jnp.dot(inner, coef, precision=HI, preferred_element_type=jnp.float32) * (1.0 / 2048.0)
    outer = (((0,), (0,)), ((), ()))
    gram[...] = lax.dot_general(coef, right, outer, precision=HI, preferred_element_type=jnp.float32)
    mine = across(place[0])
    full[...] = lax.dot_general(mine, coef, outer, precision=HI, preferred_element_type=jnp.float32)
    for m in range(2):
        for x in range(2):
            sketch[m, 0, x : x + 1, :] = full[pl.ds(place[1] + 32 * m + x, 1), :]


def finish(place, rows):
    vmem = pl.BlockSpec(memory_space=pltpu.VMEM)
    return pl.pallas_call(
        finish_kernel,
        out_shape=(
            jax.ShapeDtypeStruct((2, 1, 2, 256), jnp.float32),
            jax.ShapeDtypeStruct((256, 256), jnp.float32),
        ),
        in_specs=[pl.BlockSpec(memory_space=pltpu.SMEM), vmem],
        out_specs=(vmem, vmem),
        scratch_shapes=[pltpu.VMEM((128, 256), jnp.float32)],
        name="finish",
    )(place, rows)


def per_device(velocity, plane_count, inv_span, kernels, omega_block, omega_table, omega_stream, wall_shear):
    planes = lax.axis_size(("z", "core"))
    chips, snaps = lax.axis_size("z"), lax.axis_size("snap")
    snap, z, core = lax.axis_index("snap"), lax.axis_index("z"), lax.axis_index("core")
    flags = jnp.stack([plane_count[0], core, z % 2]).astype(jnp.float32)
    own = jnp.concatenate(
        [
            inv_span.reshape(-1),
            omega_block.reshape(-1).astype(jnp.float32),
            flags,
            jnp.zeros((53,), jnp.float32),
            kernels.reshape(-1),
            jnp.zeros((10,), jnp.float32),
        ]
    )
    inner = lax.ppermute(own, ("z", "core"), [(p, p ^ 1) for p in range(planes)])
    outer = lax.ppermute(
        own, ("z", "core"), [(p, p + 1 if p % 2 else p - 1) for p in range(1, planes - 1)]
    )
    sent = project(
        own,
        inner,
        outer,
        velocity.reshape(ROWS, 128),
        omega_table.reshape(8, 288, 256),
        omega_stream,
        wall_shear.reshape(8, 128),
        chips,
    )
    got = lax.all_to_all(sent, "z", 0, 0, tiled=True)
    sent = merge(got.reshape(chips * 8, 128), snaps * 2)
    got = lax.all_to_all(sent, ("snap", "core"), 0, 0, tiled=True)
    place = jnp.stack([16 * core + z // 2, (z % 2) * 64 + 2 * snap]).astype(jnp.int32)
    return finish(place, got.reshape(snaps * 2 * 16, 128))


def solution(mesh):
    chips = mesh.shape["plane"] // 2
    fine = Mesh(mesh.devices.reshape(mesh.shape["snap"], chips, 2), ("snap", "z", "core"))
    plane = ("z", "core")
    return jax.shard_map(
        per_device,
        mesh=fine,
        in_specs=(
            P("snap", plane, None, None, None),
            P(plane),
            P(plane, None),
            P(),
            P(plane, None),
            P(),
            P(),
            P("snap", None, plane, None),
        ),
        out_specs=(P(None, plane, "snap", None), P()),
        check_vma=False,
    )
```

time: 791 us -> 65.3 us (0.08)
  waiting for transfers between devices: 579 us -> 8.98 us
  local copies, waits for them, and re-layouts: 87.4 us -> 2.81 us
  other arithmetic: 40.9 us -> 1.39 us
  blocking collectives: 47 us -> 23.5 us
  between operations: 23.3 us -> 1.38 us
  starting transfers between devices: 10.7 us -> 18.8 us
  Pallas kernels: 0 us -> 8.02 us
    psum x1 -> x0, waiting for transfers between devices: 469 us -> none  [per_device(): gram = lax.psum(local_gram, ('snap', 'plane')) / jnp.float32(total_rows)]
    unnamed x3 -> x0, waiting for transfers between devices: 109 us -> none
    another operation x8 -> x1, local copies, waits for them, and re-layouts: 83.7 us -> 0.01 us  [the longest x4 83.6 us: features(): filtered = grads.reshape(snaps, 9, zw // 4, 4, xw // 4, 4).mean(axis=(3, 5))]
    psum x1 -> x0, blocking collectives: 47 us -> none  [per_device(): coef = lax.psum(coef, 'plane')]
    reduce_sum x6 -> x0, other arithmetic: 31.9 us -> none  [the longest x4 31.8 us: features(): filtered = grads.reshape(snaps, 9, zw // 4, 4, xw // 4, 4).mean(axis=(3, 5))]
    all_to_all x0 -> x1, blocking collectives: none -> 23.5 us  [per_device(): got = lax.all_to_all(sent, 'z', 0, 0, tiled=True)]
    all_to_all x0 -> x1, starting transfers between devices: none -> 9.38 us  [per_device(): got = lax.all_to_all(sent, ('snap', 'core'), 0, 0, tiled=True)]
    all_to_all x0 -> x1, waiting for transfers between devices: none -> 8.2 us  [per_device(): got = lax.all_to_all(sent, ('snap', 'core'), 0, 0, tiled=True)]
  transfers between devices with their start and end apart: 4 -> 3, of which waited for: 2 -> 2; matrix products, arithmetic and copies ran while one was open for 1% -> 1% of each run, Pallas kernels for 0% -> 0%
where the time goes in v1:
time: 65.3 us; the launch traced here: 64.8 us
  blocking collectives  23.5 us (36%)
  starting transfers between devices  18.8 us (29%)
  waiting for transfers between devices  8.98 us (14%)
  Pallas kernels  8.02 us (12%)
  local copies, waits for them, and re-layouts  2.81 us (4%)
  other arithmetic  1.39 us (2%)
  between operations  1.38 us (2%)
    all_to_all x1, blocking collectives, per_device(): got = lax.all_to_all(sent, 'z', 0, 0, tiled=True)  23.5 us
    all_to_all x1, starting transfers between devices, per_device(): got = lax.all_to_all(sent, ('snap', 'core'), 0, 0, tiled=True)  9.38 us
    all_to_all x1, waiting for transfers between devices, per_device(): got = lax.all_to_all(sent, ('snap', 'core'), 0, 0, tiled=True)  8.2 us
    ppermute x1, starting transfers between devices, per_device(): lax.ppermute(own, ('z', 'core'), [(p, p + 1 if p % 2 else p - 1) for p in...  4.91 us
    ppermute x1, starting transfers between devices, per_device(): lax.ppermute(own, ('z', 'core'), [(p, p ^ 1) for p in range(planes)])  4.48 us
    pallas_call x1, Pallas kernels, project(): pl.pallas_call(project_kernel, out_shape=jax.ShapeDtypeStruct((copies, 8,...  3.62 us
    pallas_call x1, Pallas kernels, finish(): pl.pallas_call(finish_kernel, out_shape=(jax.ShapeDtypeStruct((2, 1, 2, 2...  2.83 us
    unnamed x9, local copies, waits for them, and re-layouts  1.98 us
  transfers between devices with their start and end apart: 3, of which 2 were waited for; matrix products, arithmetic and copies ran while one was open for 1% of the time, Pallas kernels for 0%

profile of v1, /device:TPU:1, one launch (start us, length us, event | category | flops | bytes accessed | tf_op | source)
XLA Modules:
  0.0 64.8 jit_solution(11129426562088752763)
XLA Ops:
  1.3 0.7 %convert_bitcast_fusion = f32[4]{0:T(128)S(1)} fusion(s32[1,4]{1,0:T(1,128)} %param.12), kind=kLoop, calls=%fused_computation.2 | loop fusion | flops 4 | bytes 32 | tf_op jit(solution)/shard_map/convert_element_type | solution.py:224
  1.9 0.7 %copy.11 = f32[3,2,3,3]{3,2,1,0:T(4,128)S(1)} copy(f32[3,2,3,3]{3,1,2,0:T(2,128)} %param.11) | data formatting | bytes 432 | tf_op args[3]
  2.6 0.1 reshape.28
  2.8 0.1 add_convert_fusion
  2.8 0.7 %concatenate.3.own = f32[128]{0:T(128)S(1)} concatenate(f32[4]{0:T(128)} %bitcast.17, f32[4]{0:T(128)S(1)} %convert_bitcast_fusion, f32[3]{0:T(128)S(1)} %add_convert_fusion, f32[53]{0:T(128)S(1)} %broadcast_in_dim.3, f32[54]{0:T(128)S(1)} %reshape.28, f32[10]{0:T(128)S(1)} %broadcast.5), dimensions={0} | concatenate | bytes 1024 | tf_op jit(solution)/shard_map/concatenate | solution.py:221
  3.6 0.0 copy-start.1
  3.6 4.9 %collective-permute-start.1 = (f32[128]{0:T(128)S(1)}, f32[128]{0:T(128)S(1)}, u32[]{:S(2)}, u32[]{:S(2)}) collective-permute-start(f32[128]{0:T(128)S(1)} %concatenate.3.own), channel_id=1, source_target_pairs={{1,2},{2,1},{3,4},{4,3},{5,6},{6,5},{7,8},{8,7},{9,10},{10,9},{11,... | collective-permute-start | bytes 1544 | tf_op jit(solution)/shard_map/ppermute | solution.py:232
  8.5 4.5 %collective-permute-start = (f32[128]{0:T(128)S(1)}, f32[128]{0:T(128)S(1)}, u32[]{:S(2)}, u32[]{:S(2)}) collective-permute-start(f32[128]{0:T(128)S(1)} %concatenate.3.own), channel_id=1, source_target_pairs={{0,1},{1,0},{2,3},{3,2},{4,5},{5,4},{6,7},{7,6},{8,9},{9,8},{10,11... | collective-permute-start | bytes 1544 | tf_op jit(solution)/shard_map/ppermute | solution.py:231
  13.0 0.0 collective-permute-done.1.outer
  13.0 0.0 copy-start.2
  13.0 0.8 %collective-permute-done.inner = f32[128]{0:T(128)S(1)} collective-permute-done((f32[128]{0:T(128)S(1)}, f32[128]{0:T(128)S(1)}, u32[]{:S(2)}, u32[]{:S(2)}) %collective-permute-start) | collective-permute-done | bytes 544 | tf_op jit(solution)/shard_map/ppermute | solution.py:231
  13.8 0.0 copy-start.3
  13.8 0.0 copy-done.1
  13.8 0.0 copy-done.2
  13.8 0.6 copy-done.3
  14.4 3.6 %project.1 = f32[16,8,128]{2,1,0:T(8,128)} custom-call(f32[128]{0:T(128)} %copy-done.1, f32[128]{0:T(128)} %copy-done.3, f32[128]{0:T(128)} %copy-done.2, bf16[1536,128]{1,0:T(8,128)(2,1)} %bitcast.14, bf16[8,288,256]{2,1,0:T(8,128)(2,1)} %bitcast.12, bf16[32,256]{1,0:T(8,128)(2,1)} %stream.1, bf16[8,128]{1,0:T(8,128)(2,1)} %bitcast.16), custom_call_target="tpu_custom_call" | custom-call | tf_op jit(solution)/shard_map/project/pallas_call | solution.py:147
  18.0 23.5 %all_to_all.10 = f32[16,8,128]{2,1,0:T(8,128)} all-to-all(f32[16,8,128]{2,1,0:T(8,128)} %project.1), channel_id=1, replica_groups=mesh['snap'=16,'z'=16,'core'=2] {'z'}, dimensions={0} | all-to-all | bytes 131072 | tf_op jit(solution)/shard_map/all_to_all | solution.py:245
  41.5 1.6 %merge.1 = f32[32,16,128]{2,1,0:T(8,128)} custom-call(f32[128,128]{1,0:T(8,128)} %bitcast.15), custom_call_target="tpu_custom_call" | custom-call | tf_op jit(solution)/shard_map/merge/pallas_call | solution.py:175
  43.0 9.4 %all-to-all-start.1 = ((f32[32,16,128]{2,1,0:T(8,128)}), f32[32,16,128]{2,1,0:T(8,128)S(1)}, u32[]{:S(2)}, u32[]{:S(2)}) async-start(f32[32,16,128]{2,1,0:T(8,128)} %merge.1), calls=%async_computation.1 | async-start | bytes 524288 | tf_op jit(solution)/shard_map/all_to_all | solution.py:247
  52.4 0.6 %pad_add_fusion.place = s32[2]{0:T(128)} fusion(s32[1]{0:T(128)} %bitcast.1, s32[1]{0:T(128)} %bitcast), kind=kLoop, calls=%fused_computation | loop fusion | flops 2 | bytes 16 | tf_op jit(solution)/shard_map/stack | solution.py:248
  53.1 8.2 %all-to-all-done.1 = f32[32,16,128]{2,1,0:T(8,128)S(1)} async-done(((f32[32,16,128]{2,1,0:T(8,128)}), f32[32,16,128]{2,1,0:T(8,128)S(1)}, u32[]{:S(2)}, u32[]{:S(2)}) %all-to-all-start.1) | async-done | bytes 262176 | tf_op jit(solution)/shard_map/all_to_all | solution.py:247
  61.3 0.0 copy-start
  61.3 0.7 %copy-done = f32[32,16,128]{2,1,0:T(8,128)} copy-done((f32[32,16,128]{2,1,0:T(8,128)}, f32[32,16,128]{2,1,0:T(8,128)S(1)}, u32[]{:S(2)}) %copy-start) | copy-done | bytes 262168
  62.0 2.8 %finish.1 = (f32[2,1,2,256]{3,2,1,0:T(2,128)}, f32[256,256]{1,0:T(8,128)}) custom-call(s32[2]{0:T(128)} %pad_add_fusion.place, f32[512,128]{1,0:T(8,128)} %bitcast.13), custom_call_target="tpu_custom_call" | custom-call | tf_op jit(solution)/shard_map/finish/pallas_call | solution.py:203
  (2 shorter events, 0.0 us)
Async XLA Ops:
  3.6 10.2 %copy-start.1 = (f32[128]{0:T(128)}, f32[128]{0:T(128)S(1)}, u32[]{:S(2)}) copy-start(f32[128]{0:T(128)S(1)} %concatenate.3.own) | copy-start | bytes 1540
  3.6 9.4 %collective-permute-start.1 = (f32[128]{0:T(128)S(1)}, f32[128]{0:T(128)S(1)}, u32[]{:S(2)}, u32[]{:S(2)}) collective-permute-start(f32[128]{0:T(128)S(1)} %concatenate.3.own), channel_id=1, source_target_pairs={{1,2},{2,1},{3,4},{4,3},{5,6},{6,5},{7,8},{8,7},{9,10},{10,9},{11,... | collective-permute-start | bytes 1544 | tf_op jit(solution)/shard_map/ppermute | solution.py:232
  8.5 5.3 %collective-permute-start = (f32[128]{0:T(128)S(1)}, f32[128]{0:T(128)S(1)}, u32[]{:S(2)}, u32[]{:S(2)}) collective-permute-start(f32[128]{0:T(128)S(1)} %concatenate.3.own), channel_id=1, source_target_pairs={{0,1},{1,0},{2,3},{3,2},{4,5},{5,4},{6,7},{7,6},{8,9},{9,8},{10,11... | collective-permute-start | bytes 1544 | tf_op jit(solution)/shard_map/ppermute | solution.py:231
  13.0 0.8 %copy-start.2 = (f32[128]{0:T(128)}, f32[128]{0:T(128)S(1)}, u32[]{:S(2)}) copy-start(f32[128]{0:T(128)S(1)} %collective-permute-done.1.outer) | copy-start | bytes 1540
  13.8 0.6 copy-start.3
  43.0 18.3 %all-to-all-start.1 = ((f32[32,16,128]{2,1,0:T(8,128)}), f32[32,16,128]{2,1,0:T(8,128)S(1)}, u32[]{:S(2)}, u32[]{:S(2)}) async-start(f32[32,16,128]{2,1,0:T(8,128)} %merge.1), calls=%async_computation.1 | async-start | bytes 524288 | tf_op jit(solution)/shard_map/all_to_all | solution.py:247
  61.3 0.7 %copy-start = (f32[32,16,128]{2,1,0:T(8,128)}, f32[32,16,128]{2,1,0:T(8,128)S(1)}, u32[]{:S(2)}) copy-start(f32[32,16,128]{2,1,0:T(8,128)S(1)} %all-to-all-done.1) | copy-start | bytes 786436

commit v2 on v1

--- a/solution.py
+++ b/solution.py
@@ -10,6 +10,8 @@
 PAD = 8
 SMALL = 1.0 / 16.0
 HI = lax.Precision.HIGHEST
+LONG = pl.CostEstimate(flops=10**10, bytes_accessed=10**7, transcendentals=0)
+GRANT = pltpu.CompilerParams(vmem_limit_bytes=8 << 20)
 
 
 def iota(shape, dim):
@@ -22,19 +24,45 @@
     return high, low
 
 
-def project_kernel(own, inner, outer, vel_hbm, table_hbm, stream, shear, out, vel, table, pooled, vsem, tsem):
-    copies = []
-    for c in range(CAP):
-        part = pl.ds(c * 384, 384)
-        copy = pltpu.make_async_copy(vel_hbm.at[part], vel.at[part], vsem.at[c])
-        copy.start()
-        copies.append(copy)
-    table_copy = pltpu.make_async_copy(table_hbm, table, tsem)
-    table_copy.start()
-
+def blank_kernel(out):
+    out[...] = jnp.zeros((1, 128), jnp.float32)
+
+
+def blank():
+    return pl.pallas_call(
+        blank_kernel,
+        out_shape=jax.ShapeDtypeStruct((1, 128), jnp.float32),
+        out_specs=pl.BlockSpec(memory_space=pltpu.VMEM),
+        compiler_params=GRANT,
+        cost_estimate=LONG,
+        name="blank",
+    )()
+
+
+def pack_kernel(count, base, spans, blocks, out):
+    at = iota((1, 128), 1)
+    out[...] = base[...] + jnp.where(at == 8, count[0].astype(jnp.float32), 0.0)
+    out[0:1, 0:CAP] = spans[...]
+    out[0:1, CAP : 2 * CAP] = blocks[...].astype(jnp.float32)
+
+
+def pack(count, spans, blocks):
+    vmem = pl.BlockSpec(memory_space=pltpu.VMEM)
+    return pl.pallas_call(
+        pack_kernel,
+        out_shape=jax.ShapeDtypeStruct((1, 128), jnp.float32),
+        in_specs=[pl.BlockSpec(memory_space=pltpu.SMEM), vmem, vmem, vmem],
+        out_specs=vmem,
+        compiler_params=GRANT,
+        cost_estimate=LONG,
+        name="pack",
+    )(count, blank(), spans, blocks).reshape(128)
+
+
+def project_kernel(place, own, inner, outer, taps_in, vel, table, stream, shear, out, pooled):
     count = own[8].astype(jnp.int32)
-    odd = own[9] > 0.5
-    far = own[10] > 0.5
+    odd = place[0] == 1
+    far = place[1] % 2 == 1
 
     def pick(low, high):
         return jnp.where(odd, low, high)
@@ -54,8 +82,8 @@
     group = iota((8, 128), 1) // 32
 
     def tap(i, q, a):
-        at = 64 + ((i * 2 + q) * 3 + a) * 3
-        picked = jnp.where(group == 0, own[at], jnp.where(group == 1, own[at + 1], own[at + 2]))
+        at = ((i * 2 + q) * 3 + a) * 3
+        picked = jnp.where(group == 0, taps_in[at], jnp.where(group == 1, taps_in[at + 1], taps_in[at + 2]))
         return jnp.where(group < 3, picked * SMALL, 0.0)
 
     taps = {(i, q, a): tap(i, q, a) for i in range(3) for q in range(2) for a in range(3)}
@@ -68,7 +96,6 @@
 
     planes, normals = [], []
     for c in range(CAP):
-        copies[c].wait()
         pooled[pl.ds(PAD + c * 384, 384), :] = jnp.dot(
             vel[pl.ds(c * 384, 384), :], pool, preferred_element_type=jnp.float32
         )
@@ -96,7 +123,6 @@
             jnp.dot(jnp.concatenate(centres, axis=0), centre, preferred_element_type=jnp.float32)
         )
 
-    table_copy.wait()
     total = jnp.zeros((8, 256), jnp.float32)
 
     def rows_of(block, channel):
@@ -140,24 +166,20 @@
         out[copy_at] = tile
 
 
-def project(own, inner, outer, velocity, table, stream, shear, copies):
+def project(place, own, inner, outer, taps, velocity, table, stream, shear, copies):
     smem = pl.BlockSpec(memory_space=pltpu.SMEM)
     vmem = pl.BlockSpec(memory_space=pltpu.VMEM)
-    hbm = pl.BlockSpec(memory_space=pl.ANY)
     return pl.pallas_call(
         project_kernel,
         out_shape=jax.ShapeDtypeStruct((copies, 8, 128), jnp.float32),
-        in_specs=[smem, smem, smem, hbm, hbm, vmem, vmem],
+        in_specs=[smem, smem, smem, smem, smem, vmem, vmem, vmem, vmem],
         out_specs=vmem,
         scratch_shapes=[
-            pltpu.VMEM((ROWS, 128), jnp.bfloat16),
-            pltpu.VMEM((8, 288, 256), jnp.bfloat16),
             pltpu.VMEM((ROWS + 2 * PAD, 128), jnp.float32),
-            pltpu.SemaphoreType.DMA((CAP,)),
-            pltpu.SemaphoreType.DMA,
         ],
+        compiler_params=GRANT,
         name="project",
-    )(own, inner, outer, velocity, table, stream, shear)
+    )(place, own, inner, outer, taps, velocity, table, stream, shear)
 
 
 def merge_kernel(rows, out):
@@ -177,6 +199,7 @@
         out_shape=jax.ShapeDtypeStruct((copies, 16, 128), jnp.float32),
         in_specs=[pl.BlockSpec(memory_space=pltpu.VMEM)],
         out_specs=pl.BlockSpec(memory_space=pltpu.VMEM),
+        compiler_params=GRANT,
         name="merge",
     )(rows)
 
@@ -191,11 +214,13 @@
     right = jnp.dot(inner, coef, precision=HI, preferred_element_type=jnp.float32) * (1.0 / 2048.0)
     outer = (((0,), (0,)), ((), ()))
     gram[...] = lax.dot_general(coef, right, outer, precision=HI, preferred_element_type=jnp.float32)
-    mine = across(place[0])
+    core, chip, snap = place[0], place[1], place[2]
+    mine = across(16 * core + chip // 2)
+    base = (chip % 2) * 64 + 2 * snap
     full[...] = lax.dot_general(mine, coef, outer, precision=HI, preferred_element_type=jnp.float32)
     for m in range(2):
         for x in range(2):
-            sketch[m, 0, x : x + 1, :] = full[pl.ds(place[1] + 32 * m + x, 1), :]
+            sketch[m, 0, x : x + 1, :] = full[pl.ds(base + 32 * m + x, 1), :]
 
 
 def finish(place, rows):
@@ -209,6 +234,7 @@
         in_specs=[pl.BlockSpec(memory_space=pltpu.SMEM), vmem],
         out_specs=(vmem, vmem),
         scratch_shapes=[pltpu.VMEM((128, 256), jnp.float32)],
+        compiler_params=GRANT,
         name="finish",
     )(place, rows)
 
@@ -217,25 +243,18 @@
     planes = lax.axis_size(("z", "core"))
     chips, snaps = lax.axis_size("z"), lax.axis_size("snap")
     snap, z, core = lax.axis_index("snap"), lax.axis_index("z"), lax.axis_index("core")
-    flags = jnp.stack([plane_count[0], core, z % 2]).astype(jnp.float32)
-    own = jnp.concatenate(
-        [
-            inv_span.reshape(-1),
-            omega_block.reshape(-1).astype(jnp.float32),
-            flags,
-            jnp.zeros((53,), jnp.float32),
-            kernels.reshape(-1),
-            jnp.zeros((10,), jnp.float32),
-        ]
-    )
+    own = pack(plane_count, inv_span, omega_block)
     inner = lax.ppermute(own, ("z", "core"), [(p, p ^ 1) for p in range(planes)])
     outer = lax.ppermute(
         own, ("z", "core"), [(p, p + 1 if p % 2 else p - 1) for p in range(1, planes - 1)]
     )
+    place = jnp.stack([core, z, snap]).astype(jnp.int32)
     sent = project(
+        place,
         own,
         inner,
         outer,
+        kernels.reshape(-1),
         velocity.reshape(ROWS, 128),
         omega_table.reshape(8, 288, 256),
         omega_stream,
@@ -245,7 +264,6 @@
     got = lax.all_to_all(sent, "z", 0, 0, tiled=True)
     sent = merge(got.reshape(chips * 8, 128), snaps * 2)
     got = lax.all_to_all(sent, ("snap", "core"), 0, 0, tiled=True)
-    place = jnp.stack([16 * core + z // 2, (z % 2) * 64 + 2 * snap]).astype(jnp.int32)
     return finish(place, got.reshape(snaps * 2 * 16, 128))
 
 

time: 65.3 us -> 56.9 us (0.87)
  blocking collectives: 23.5 us -> 41.2 us
  starting transfers between devices: 18.8 us -> 9.53 us
  waiting for transfers between devices: 8.98 us -> 0.6 us
  Pallas kernels: 8.02 us -> 3.76 us
  local copies, waits for them, and re-layouts: 2.81 us -> 0.14 us
  other arithmetic: 1.39 us -> 0.08 us
    all_to_all x0 -> x1, blocking collectives: none -> 18.1 us  [per_device(): got = lax.all_to_all(sent, ('snap', 'core'), 0, 0, tiled=True)]
    all_to_all x1 -> x0, starting transfers between devices: 9.38 us -> none  [per_device(): got = lax.all_to_all(sent, ('snap', 'core'), 0, 0, tiled=True)]
    all_to_all x1 -> x0, waiting for transfers between devices: 8.2 us -> none  [per_device(): got = lax.all_to_all(sent, ('snap', 'core'), 0, 0, tiled=True)]
    pallas_call x1, Pallas kernels: 3.62 us -> 1.25 us  [project(): pl.pallas_call(project_kernel, out_shape=jax.ShapeDtypeStruct((copies, 8,...]
    unnamed x9 -> x15, local copies, waits for them, and re-layouts: 1.98 us -> 0.04 us
    pallas_call x1, Pallas kernels: 1.56 us -> 0.02 us  [merge(): pl.pallas_call(merge_kernel, out_shape=jax.ShapeDtypeStruct((copies, 16,...]
    convert_element_type x2 -> x0, other arithmetic: 0.74 us -> none  [the longest x1 0.66 us: per_device(): omega_block.reshape(-1).astype(jnp.float32)]
    concatenate x1 -> x0, local copies, waits for them, and re-layouts: 0.73 us -> none  [per_device(): jnp.concatenate([inv_span.reshape(-1), omega_block.reshape(-1).astype(jnp...]
  transfers between devices with their start and end apart: 3 -> 2, of which waited for: 2 -> 1; matrix products, arithmetic and copies ran while one was open for 1% -> 0% of each run, Pallas kernels for 0% -> 0%
where the time goes in v2:
time: 56.9 us; the launch traced here: 56.7 us
  blocking collectives  41.2 us (72%)
  starting transfers between devices  9.53 us (17%)
  Pallas kernels  3.76 us (7%)
  between operations  1.41 us (2%)
  waiting for transfers between devices  0.6 us (1%)
    all_to_all x1, blocking collectives, per_device(): got = lax.all_to_all(sent, 'z', 0, 0, tiled=True)  23.1 us
    all_to_all x1, blocking collectives, per_device(): got = lax.all_to_all(sent, ('snap', 'core'), 0, 0, tiled=True)  18.1 us
    ppermute x1, starting transfers between devices, per_device(): lax.ppermute(own, ('z', 'core'), [(p, p + 1 if p % 2 else p - 1) for p in...  5.04 us
    ppermute x1, starting transfers between devices, per_device(): lax.ppermute(own, ('z', 'core'), [(p, p ^ 1) for p in range(planes)])  4.48 us
    pallas_call x1, Pallas kernels, finish(): pl.pallas_call(finish_kernel, out_shape=(jax.ShapeDtypeStruct((2, 1, 2, 2...  2.41 us
    pallas_call x1, Pallas kernels, project(): pl.pallas_call(project_kernel, out_shape=jax.ShapeDtypeStruct((copies, 8,...  1.25 us
  transfers between devices with their start and end apart: 2, of which 1 were waited for; matrix products, arithmetic and copies ran while one was open for 0% of the time, Pallas kernels for 0%

profile of v2, /device:TPU:1, one launch (start us, length us, event | category | flops | bytes accessed | tf_op | source)
XLA Modules:
  0.0 56.7 jit_solution(13923417743702886648)
XLA Ops:
  0.6 0.0 copy-start.5
  0.6 0.0 copy-start.4
  1.3 0.0 copy-done.5
  1.3 0.0 copy-done.4
  1.3 0.0 copy-start.6
  1.3 0.0 copy-start
  1.4 0.0 copy-start.1
  1.4 0.0 copy-start.2
  1.4 0.0 copy-start.3
  1.4 0.1 pack.1
  1.5 5.0 %collective-permute-start.1 = (f32[128]{0:T(128)S(1)}, f32[128]{0:T(128)S(1)}, u32[]{:S(2)}, u32[]{:S(2)}) collective-permute-start(f32[128]{0:T(128)S(1)} %bitcast.14), channel_id=1, source_target_pairs={{1,2},{2,1},{3,4},{4,3},{5,6},{6,5},{7,8},{8,7},{9,10},{10,9},{11,... | collective-permute-start | bytes 1544 | tf_op jit(solution)/shard_map/ppermute | solution.py:248
  6.5 4.5 %collective-permute-start = (f32[128]{0:T(128)S(1)}, f32[128]{0:T(128)S(1)}, u32[]{:S(2)}, u32[]{:S(2)}) collective-permute-start(f32[128]{0:T(128)S(1)} %bitcast.15), channel_id=1, source_target_pairs={{0,1},{1,0},{2,3},{3,2},{4,5},{5,4},{6,7},{7,6},{8,9},{9,8},{10,11... | collective-permute-start | bytes 1544 | tf_op jit(solution)/shard_map/ppermute | solution.py:247
  11.0 0.1 pad_add_fusion.place
  11.1 0.0 copy-done.6
  11.1 0.1 reshape.26.taps_in
  11.2 0.0 collective-permute-done.1.outer
  11.2 0.6 %collective-permute-done.inner = f32[128]{0:T(128)S(1)} collective-permute-done((f32[128]{0:T(128)S(1)}, f32[128]{0:T(128)S(1)}, u32[]{:S(2)}, u32[]{:S(2)}) %collective-permute-start) | collective-permute-done | bytes 544 | tf_op jit(solution)/shard_map/ppermute | solution.py:247
  11.8 0.0 copy-done
  11.8 0.0 copy-done.1
  11.8 0.0 copy-done.2
  11.8 0.0 copy-done.3
  11.8 1.3 %project.1 = f32[16,8,128]{2,1,0:T(8,128)S(1)} custom-call(s32[3]{0:T(128)S(1)} %pad_add_fusion.place, f32[128]{0:T(128)S(1)} %bitcast.16, f32[128]{0:T(128)S(1)} %collective-permute-done.inner, f32[128]{0:T(128)S(1)} %collective-permute-done.1.outer, f32[54]{0:T(128)S(1)} %reshape.26.taps_in, bf16[1536,128]{1,0:T(8,128)(2,1)S(1)} %bitcast.11, ...), custom_call_target="tpu_custom_call" | custom-call | tf_op jit(solution)/shard_map/project/pallas_call | solution.py:172
  13.1 23.1 %all_to_all.10 = f32[16,8,128]{2,1,0:T(8,128)S(1)} all-to-all(f32[16,8,128]{2,1,0:T(8,128)S(1)} %project.1), channel_id=1, replica_groups=mesh['snap'=16,'z'=16,'core'=2] {'z'}, dimensions={0} | all-to-all | bytes 131072 | tf_op jit(solution)/shard_map/all_to_all | solution.py:264
  36.3 18.1 %all_to_all.11 = f32[32,16,128]{2,1,0:T(8,128)S(1)} all-to-all(f32[32,16,128]{2,1,0:T(8,128)S(1)} %merge.1), channel_id=1, replica_groups=mesh['snap'=16,'z'=16,'core'=2] {'snap','core'}, dimensions={0} | all-to-all | bytes 524288 | tf_op jit(solution)/shard_map/all_to_all | solution.py:266
  54.3 2.4 %finish.1 = (f32[2,1,2,256]{3,2,1,0:T(2,128)}, f32[256,256]{1,0:T(8,128)}) custom-call(s32[3]{0:T(128)S(1)} %pad_add_fusion.place, f32[512,128]{1,0:T(8,128)S(1)} %bitcast.10), custom_call_target="tpu_custom_call" | custom-call | tf_op jit(solution)/shard_map/finish/pallas_call | solution.py:228
  (3 shorter events, 0.0 us)
Async XLA Ops:
  0.6 0.7 %copy-start.5 = (s32[1,4]{1,0:T(1,128)S(1)}, s32[1,4]{1,0:T(1,128)}, u32[]{:S(2)}) copy-start(s32[1,4]{1,0:T(1,128)} %blocks.1) | copy-start | bytes 52
  0.6 0.7 %copy-start.4 = (f32[1,4]{1,0:T(1,128)S(1)}, f32[1,4]{1,0:T(1,128)}, u32[]{:S(2)}) copy-start(f32[1,4]{1,0:T(1,128)} %spans.1) | copy-start | bytes 52
  1.3 9.8 %copy-start.6 = (f32[3,2,3,3]{3,1,2,0:T(2,128)S(1)}, f32[3,2,3,3]{3,1,2,0:T(2,128)}, u32[]{:S(2)}) copy-start(f32[3,2,3,3]{3,1,2,0:T(2,128)} %param.11) | copy-start | bytes 652
  1.3 10.5 %copy-start = (bf16[8,9,32,256]{3,2,1,0:T(8,128)(2,1)S(1)}, bf16[8,9,32,256]{3,2,1,0:T(8,128)(2,1)}, u32[]{:S(2)}) copy-start(bf16[8,9,32,256]{3,2,1,0:T(8,128)(2,1)} %param.13) | copy-start | bytes 3538948
  1.4 10.5 %copy-start.1 = (bf16[1,4,3,128,128]{4,3,2,1,0:T(8,128)(2,1)S(1)}, bf16[1,4,3,128,128]{4,3,2,1,0:T(8,128)(2,1)}, u32[]{:S(2)}) copy-start(bf16[1,4,3,128,128]{4,3,2,1,0:T(8,128)(2,1)} %param.8) | copy-start | bytes 1179652
  1.4 10.4 %copy-start.2 = (bf16[32,256]{1,0:T(8,128)(2,1)S(1)}, bf16[32,256]{1,0:T(8,128)(2,1)}, u32[]{:S(2)}) copy-start(bf16[32,256]{1,0:T(8,128)(2,1)} %stream.1) | copy-start | bytes 49156
  1.4 10.4 %copy-start.3 = (bf16[1,2,4,128]{3,2,1,0:T(4,128)(2,1)S(1)}, bf16[1,2,4,128]{3,2,1,0:T(4,128)(2,1)}, u32[]{:S(2)}) copy-start(bf16[1,2,4,128]{3,2,1,0:T(4,128)(2,1)} %param.15) | copy-start | bytes 6148
  1.5 9.7 %collective-permute-start.1 = (f32[128]{0:T(128)S(1)}, f32[128]{0:T(128)S(1)}, u32[]{:S(2)}, u32[]{:S(2)}) collective-permute-start(f32[128]{0:T(128)S(1)} %bitcast.14), channel_id=1, source_target_pairs={{1,2},{2,1},{3,4},{4,3},{5,6},{6,5},{7,8},{8,7},{9,10},{10,9},{11,... | collective-permute-start | bytes 1544 | tf_op jit(solution)/shard_map/ppermute | solution.py:248
  6.5 5.3 %collective-permute-start = (f32[128]{0:T(128)S(1)}, f32[128]{0:T(128)S(1)}, u32[]{:S(2)}, u32[]{:S(2)}) collective-permute-start(f32[128]{0:T(128)S(1)} %bitcast.15), channel_id=1, source_target_pairs={{0,1},{1,0},{2,3},{3,2},{4,5},{5,4},{6,7},{7,6},{8,9},{9,8},{10,11... | collective-permute-start | bytes 1544 | tf_op jit(solution)/shard_map/ppermute | solution.py:247

commit v3 on v2

v3 whole, which is shorter than its diff:
```python
import jax
import jax.numpy as jnp
from jax import lax
from jax.experimental import pallas as pl
from jax.experimental.pallas import tpu as pltpu
from jax.sharding import Mesh, PartitionSpec as P

CAP = 4
BLOCKS = 8
ROWS = 1536
PAD = 8
SENT = 24
SMALL = 1.0 / 16.0
LONG = pl.CostEstimate(flops=10**10, bytes_accessed=10**7, transcendentals=0)
GRANT = pltpu.CompilerParams(vmem_limit_bytes=8 << 20)
SMEM = pl.BlockSpec(memory_space=pltpu.SMEM)
VMEM = pl.BlockSpec(memory_space=pltpu.VMEM)
OVER_ROWS = (((0,), (0,)), ((), ()))


def iota(shape, dim):
    return lax.broadcasted_iota(jnp.int32, shape, dim)


def split(value):
    high = value.astype(jnp.bfloat16)
    low = (value - high.astype(jnp.float32)).astype(jnp.bfloat16)
    return high, low


def dot(left, right):
    return jnp.dot(left, right, preferred_element_type=jnp.float32)


def call(kernel, name, out, ins, scratch=(), cost=None):
    return pl.pallas_call(
        kernel,
        out_shape=out,
        in_specs=ins,
        out_specs=jax.tree.map(lambda _: VMEM, out),
        scratch_shapes=list(scratch),
        compiler_params=GRANT,
        cost_estimate=cost,
        name=name,
    )


def blank_kernel(out):
    out[...] = jnp.zeros((8, 128), jnp.float32)


def pack_kernel(count, spans, blocks, base, out):
    last = count[0] - 1
    row = iota((8, 128), 0)
    tile = jnp.where(row == 0, spans[0, 0], base[...])
    tile = jnp.where(row == 1, blocks[0, 0].astype(jnp.float32), tile)
    tile = jnp.where(row == 2, spans[0, last], tile)
    out[...] = jnp.where(row == 3, blocks[0, last].astype(jnp.float32), tile)


def project_kernel(place, count_in, spans, blocks, taps_in, vel, table, stream, shear, out, pooled):
    count = count_in[0]
    odd = place[0] == 1

    lane = iota((128, 128), 1)
    gap = iota((128, 128), 0) - 4 * (lane % 32) - lane // 32 + 1
    pool = jnp.where((gap >= 0) & (gap < 4) & (lane < 96), 1.0, 0.0).astype(jnp.bfloat16)
    group = iota((8, 128), 1) // 32

    def tap(i, q, a):
        at = ((i * 2 + q) * 3 + a) * 3
        picked = jnp.where(group == 0, taps_in[at], jnp.where(group == 1, taps_in[at + 1], taps_in[at + 2]))
        return jnp.where(group < 3, picked * SMALL, 0.0)

    taps = {(i, q, a): tap(i, q, a) for i in range(3) for q in range(2) for a in range(3)}
    zeros = jnp.zeros((32, 256), jnp.bfloat16)
    omega = stream[...]
    spread = jnp.concatenate([omega, zeros, zeros, zeros], axis=0)
    centre = jnp.concatenate([zeros, omega, zeros, zeros] * 2, axis=0)
    first_row = iota((32, 128), 0) == 0
    last_row = iota((32, 128), 0) == 31

    planes, normals = [], []
    for c in range(CAP):
        pooled[pl.ds(PAD + c * 384, 384), :] = dot(vel[pl.ds(c * 384, 384), :], pool)
    for c in range(CAP):
        feats, centres = [], []
        for i in range(3):
            base = PAD + (c * 3 + i) * 128
            row = [pooled[pl.ds(base + j, 32, stride=4), :] for j in range(4)]
            before = jnp.where(first_row, 0.0, pooled[pl.ds(base - 1, 32, stride=4), :])
            after = jnp.where(last_row, 0.0, pooled[pl.ds(base + 4, 32, stride=4), :])
            inside = row[1] + row[2]
            head = row[0] + inside
            window = (before + head, head + row[3], inside + row[3] + after)
            for q in range(2):
                mixed = sum(
                    (window[a].reshape(4, 8, 128) * taps[i, q, a][None]).reshape(32, 128) for a in range(3)
                )
                folded = mixed + pltpu.roll(mixed, 96, 1) + pltpu.roll(mixed, 64, 1)
                feats.append(folded.astype(jnp.bfloat16))
            centres.append(jnp.concatenate(split(window[1] * SMALL), axis=1))
        planes.append(dot(jnp.concatenate(feats, axis=0), spread))
        normals.append(dot(jnp.concatenate(centres, axis=0), centre))

    def rows_of(block, channel):
        return table[block, channel * 32 : channel * 32 + 32, :].astype(jnp.float32)

    def fold(value):
        return value.reshape(4, 8, 256).sum(0)

    total = jnp.zeros((8, 256), jnp.float32)
    for c in range(CAP):
        alive = jnp.where(c < count, 1.0, 0.0)
        part = jnp.zeros((8, 256), jnp.float32)
        for i in range(3):
            for q in range(2):
                at = (i * 2 + q) * 32
                part += fold(planes[c][at : at + 32] * rows_of(blocks[0, c], 3 * i + q))
            weight = None
            if c:
                weight = spans[0, c - 1] * rows_of(blocks[0, c - 1], 3 * i + 2)
            if c + 1 < CAP:
                span = jnp.where(c + 1 < count, spans[0, c + 1], 0.0)
                down = span * rows_of(blocks[0, c + 1], 3 * i + 2)
                weight = -down if weight is None else weight - down
            part += fold(normals[c][i * 32 : i * 32 + 32] * weight)
        total += alive * part
    out[0:8, :] = total

    final = sum(jnp.where(c + 1 == count, 1.0, 0.0) * normals[c] for c in range(CAP))
    edges = (jnp.where(odd, final, normals[0]), jnp.where(odd, normals[0], final))
    found = ([], [])
    for block in range(BLOCKS):
        parts = [jnp.zeros((8, 256), jnp.float32)] * 2
        for i in range(3):
            rows = rows_of(block, 3 * i + 2)
            parts = [part + fold(edge[i * 32 : i * 32 + 32] * rows) for part, edge in zip(parts, edges)]
        for part, rows in zip(parts, found):
            rows.append(jnp.sum(part, axis=0, keepdims=True))
    out[8:16, :] = jnp.concatenate(found[0], axis=0)
    out[16:24, :] = jnp.concatenate(found[1], axis=0)

    wall = dot(shear[...], pool) * SMALL
    first = jnp.broadcast_to(jnp.sum(wall[0:4], axis=0, keepdims=True), (8, 128))
    second = jnp.broadcast_to(jnp.sum(wall[4:8], axis=0, keepdims=True), (8, 128))
    low = jnp.where(group == 0, pltpu.roll(first, 96, 1), jnp.where(group == 1, second, 0.0))
    out[24:32, :] = jnp.concatenate([low, low], axis=1)


def send_kernel(place, part, partner, out):
    odd = place[0] == 1
    tile = partner[...]
    row = iota((8, 128), 0)

    def spread(at):
        return jnp.broadcast_to(tile[at : at + 1], (8, 128))

    span = jnp.where(odd, spread(2), -spread(0))
    block = jnp.where(odd, spread(3), spread(1)).astype(jnp.int32)
    weight = jnp.where(row == block, span, 0.0)
    near = part[16:24, :] * jnp.concatenate([weight, weight], axis=1)
    coef = jnp.sum(part[0:8, :] + near, axis=0, keepdims=True)
    coef = jnp.broadcast_to(coef, (8, 256))

    def pair(value):
        high = value.astype(jnp.bfloat16).astype(jnp.float32)
        return high, value - high

    high, low = pair(coef)
    wall, wall_low = pair(part[24:32, :128])
    wall = wall + pltpu.roll(wall_low, 64, 1)
    far, far_low = pair(jnp.where(odd, -spread(0), spread(2)))
    told = jnp.where(odd, spread(1), spread(3))
    picks = (high[:, :128], high[:, 128:], low[:, :128], low[:, 128:], wall, far, far_low, told)
    small = picks[-1]
    for at in range(7):
        small = jnp.where(row == at, picks[at], small)
    outer = part[8:16, :]
    whole = jnp.concatenate([outer[:, :128], outer[:, 128:], small], axis=0).astype(jnp.bfloat16)
    for copy_at in range(out.shape[0]):
        out[copy_at] = whole


def merge_kernel(place, rows, out, wide):
    odd = place[0] == 1
    chips = rows.shape[0] // SENT
    wide[...] = rows[...].astype(jnp.float32)

    def every(at):
        return wide[pl.ds(16 + at, chips, stride=SENT), :]

    low = jnp.sum(every(0) + every(2), axis=0, keepdims=True)
    high = jnp.sum(every(1) + every(3), axis=0, keepdims=True)
    wall = every(4)
    wall = wall + pltpu.roll(wall, 64, 1)
    sub = iota((8, 128), 0)
    reach = [jnp.zeros((8, 128), jnp.float32)] * 2
    for j in range(chips):
        span = wide[SENT * j + 21 : SENT * j + 22, :] + wide[SENT * j + 22 : SENT * j + 23, :]
        block = jnp.broadcast_to(wide[SENT * j + 23 : SENT * j + 24, :], (8, 128)).astype(jnp.int32)
        weight = jnp.where(sub == block, jnp.broadcast_to(span, (8, 128)), 0.0)
        before = wide[pl.ds(SENT * (j - 1), 16), :] if j > 0 else jnp.zeros((16, 128), jnp.float32)
        after = wide[pl.ds(SENT * (j + 1), 16), :] if j + 1 < chips else jnp.zeros((16, 128), jnp.float32)
        held = jnp.where(odd, before, after)
        reach = [reach[h] + weight * held[8 * h : 8 * h + 8] for h in range(2)]
    low = low + jnp.sum(reach[0], axis=0, keepdims=True)
    high = high + jnp.sum(reach[1], axis=0, keepdims=True)
    left = iota((8, 128), 1) < 64
    wide[0:chips, :] = wall
    wall = jnp.where(left, wide[pl.ds(0, 8, stride=2), :], wide[pl.ds(1, 8, stride=2), :])
    low = jnp.broadcast_to(low, (8, 128))
    high = jnp.broadcast_to(high, (8, 128))
    low_top = low.astype(jnp.bfloat16).astype(jnp.float32)
    high_top = high.astype(jnp.bfloat16).astype(jnp.float32)
    wall_top = wall.astype(jnp.bfloat16).astype(jnp.float32)
    small = jnp.where(sub == 0, low_top, jnp.where(sub == 1, high_top, jnp.where(sub == 2, low - low_top, jnp.where(sub == 3, high - high_top, 0.0))))
    whole = jnp.concatenate([wall_top, wall - wall_top, small], axis=0).astype(jnp.bfloat16)
    for copy_at in range(out.shape[0]):
        out[copy_at] = whole


def finish_kernel(place, rows, sketch, gram, wide, full):
    wide[...] = rows[...].astype(jnp.float32)

    def across(at):
        return wide[pl.ds(at, 16, stride=2 * SENT), :]

    def both(at):
        return across(at) + across(at + 2) + across(at + SENT) + across(at + SENT + 2)

    coef = jnp.concatenate([both(16), both(17)], axis=1)
    coef_high, coef_low = split(coef)
    walls = [
        jnp.concatenate([across(at), across(at + 8)], axis=0).astype(jnp.bfloat16)
        for at in [SENT * core + r for core in range(2) for r in range(8)]
    ]
    wall = jnp.concatenate(walls, axis=1)
    product = lax.dot_general(wall, wall, (((1,), (1,)), ((), ())), preferred_element_type=jnp.float32)
    product = product[0:16] + product[16:32]
    inner = product[:, 0:16] + product[:, 16:32]
    inner_high, inner_low = split(inner)
    right = dot(inner_high, coef_high) + dot(inner_low, coef_high) + dot(inner_high, coef_low)
    right_high, right_low = split(right * (1.0 / 2048.0))
    left = jnp.concatenate([coef_high, coef_low, coef_high], axis=0)
    gram[...] = lax.dot_general(
        left,
        jnp.concatenate([right_high, right_high, right_low], axis=0),
        OVER_ROWS,
        preferred_element_type=jnp.float32,
    )
    core, chip, snap = place[0], place[1], place[2]
    at = SENT * core + chip // 2
    mine_high = across(at).astype(jnp.bfloat16)
    mine_low = across(at + 8).astype(jnp.bfloat16)
    mine = jnp.concatenate([mine_high, mine_high, mine_low], axis=0)
    full[...] = lax.dot_general(mine, left, OVER_ROWS, preferred_element_type=jnp.float32)
    base = (chip % 2) * 64 + 2 * snap
    for m in range(2):
        for x in range(2):
            sketch[m, 0, x : x + 1, :] = full[pl.ds(base + 32 * m + x, 1), :]


def per_device(velocity, plane_count, inv_span, kernels, omega_block, omega_table, omega_stream, wall_shear):
    f32, bf16 = jnp.float32, jnp.bfloat16
    chips, snaps = lax.axis_size("z"), lax.axis_size("snap")
    snap, z, core = lax.axis_index("snap"), lax.axis_index("z"), lax.axis_index("core")
    place = jnp.stack([core, z, snap]).astype(jnp.int32)
    tile = jax.ShapeDtypeStruct((8, 128), f32)
    base = call(blank_kernel, "blank", tile, [], cost=LONG)()
    own = call(pack_kernel, "pack", tile, [SMEM, SMEM, SMEM, VMEM], cost=LONG)(
        plane_count, inv_span, omega_block, base
    )
    partner = lax.ppermute(own, "core", [(0, 1), (1, 0)])
    part = call(
        project_kernel,
        "project",
        jax.ShapeDtypeStruct((32, 256), f32),
        [SMEM] * 5 + [VMEM] * 4,
        [pltpu.VMEM((ROWS + 2 * PAD, 128), f32)],
        cost=LONG,
    )(
        place,
        plane_count,
        inv_span,
        omega_block,
        kernels.reshape(-1),
        velocity.reshape(ROWS, 128),
        omega_table.reshape(BLOCKS, 288, 256),
        omega_stream,
        wall_shear.reshape(8, 128),
    )
    sent = call(send_kernel, "send", jax.ShapeDtypeStruct((chips, SENT, 128), bf16), [SMEM, VMEM, VMEM])(
        place, part, partner
    )
    got = lax.all_to_all(sent, "z", 0, 0, tiled=True).reshape(chips * SENT, 128)
    sent = call(
        merge_kernel,
        "merge",
        jax.ShapeDtypeStruct((snaps * 2, SENT, 128), bf16),
        [SMEM, VMEM],
        [pltpu.VMEM((chips * SENT, 128), f32)],
    )(place, got)
    got = lax.all_to_all(sent, ("snap", "core"), 0, 0, tiled=True).reshape(snaps * 2 * SENT, 128)
    return call(
        finish_kernel,
        "finish",
        (jax.ShapeDtypeStruct((2, 1, 2, 256), f32), jax.ShapeDtypeStruct((256, 256), f32)),
        [SMEM, VMEM],
        [pltpu.VMEM((snaps * 2 * SENT, 128), f32), pltpu.VMEM((128, 256), f32)],
    )(place, got)


def solution(mesh):
    chips = mesh.shape["plane"] // 2
    fine = Mesh(mesh.devices.reshape(mesh.shape["snap"], chips, 2), ("snap", "z", "core"))
    plane = ("z", "core")
    return jax.shard_map(
        per_device,
        mesh=fine,
        in_specs=(
            P("snap", plane, None, None, None),
            P(plane),
            P(plane, None),
            P(),
            P(plane, None),
            P(),
            P(),
            P("snap", None, plane, None),
        ),
        out_specs=(P(None, plane, "snap", None), P()),
        check_vma=False,
    )
```

time: 56.9 us -> 54 us (0.949)
  blocking collectives: 41.2 us -> 38.2 us
  Pallas kernels: 3.76 us -> 5.13 us
  starting transfers between devices: 9.53 us -> 8.75 us
  waiting for transfers between devices: 0.6 us -> 0.01 us
    all_to_all x2, blocking collectives: 41.2 us -> 38.2 us  [the longest x1 21.4 us: per_device(): got = lax.all_to_all(sent, 'z', 0, 0, tiled=True).reshape(chips * SENT, 128)]
    pallas_call x5 -> x6, Pallas kernels: 3.76 us -> 5.13 us  [the longest x1 1.89 us: per_device(): call(finish_kernel, 'finish', (jax.ShapeDtypeStruct((2, 1, 2, 256), f32),...]
    ppermute x2 -> x1, starting transfers between devices: 9.53 us -> 8.75 us  [per_device(): partner = lax.ppermute(own, 'core', [(0, 1), (1, 0)])]
    ppermute x2 -> x1, waiting for transfers between devices: 0.6 us -> 0.01 us  [per_device(): partner = lax.ppermute(own, 'core', [(0, 1), (1, 0)])]
  transfers between devices with their start and end apart: 2 -> 1, of which waited for: 1 -> 0; matrix products, arithmetic and copies ran while one was open for 0% -> 0% of each run, Pallas kernels for 0% -> 3%
where the time goes in v3:
time: 54 us; the launch traced here: 53.8 us
  blocking collectives  38.2 us (71%)
  starting transfers between devices  8.75 us (16%)
  Pallas kernels  5.13 us (10%)
  between operations  1.42 us (3%)
    all_to_all x1, blocking collectives, per_device(): got = lax.all_to_all(sent, 'z', 0, 0, tiled=True).reshape(chips * SENT, 128)  21.4 us
    all_to_all x1, blocking collectives, per_device(): lax.all_to_all(sent, ('snap', 'core'), 0, 0, tiled=True)  16.9 us
    ppermute x1, starting transfers between devices, per_device(): partner = lax.ppermute(own, 'core', [(0, 1), (1, 0)])  8.75 us
    pallas_call x1, Pallas kernels, per_device(): call(finish_kernel, 'finish', (jax.ShapeDtypeStruct((2, 1, 2, 256), f32),...  1.89 us
    pallas_call x1, Pallas kernels, per_device(): call(project_kernel, 'project', jax.ShapeDtypeStruct((32, 256), f32), [SM...  1.42 us
  transfers between devices with their start and end apart: 1, of which 0 were waited for; matrix products, arithmetic and copies ran while one was open for 0% of the time, Pallas kernels for 3%

profile of v3, /device:TPU:1, one launch (start us, length us, event | category | flops | bytes accessed | tf_op | source)
XLA Modules:
  0.0 53.8 jit_solution(8828246711414435257)
XLA Ops:
  0.6 0.0 copy-start.5
  0.6 0.0 copy-start.4
  1.3 0.0 copy-done.5
  1.3 0.0 copy-done.4
  1.3 0.0 copy-start.6
  1.3 0.0 copy-start
  1.4 0.0 copy-start.1
  1.4 0.0 copy-start.2
  1.4 0.0 copy-start.3
  1.4 0.6 %pack.1 = f32[8,128]{1,0:T(8,128)S(1)} custom-call(s32[1]{0:T(128)S(6)} %copy.12.count_in.count, f32[1,4]{1,0:T(1,128)S(1)} %copy-done.4, s32[1,4]{1,0:T(1,128)S(1)} %copy-done.5, f32[8,128]{1,0:T(8,128)S(1)} %blank.1.base), custom_call_target="tpu_custom_call" | custom-call | flops 10000000000 | bytes 10000000 | tf_op jit(solution)/shard_map/pack/pallas_call | solution.py:271
  2.0 8.7 %collective-permute-start = (f32[8,128]{1,0:T(8,128)S(1)}, f32[8,128]{1,0:T(8,128)S(1)}, u32[]{:S(2)}, u32[]{:S(2)}) collective-permute-start(f32[8,128]{1,0:T(8,128)S(1)} %pack.1), channel_id=1, source_target_pairs={{0,1},{1,0},{2,3},{3,2},{4,5},{5,4},{6,7},{7,6},{8,9},{9,8},{10,11... | collective-permute-start | bytes 12296 | tf_op jit(solution)/shard_map/ppermute | solution.py:274
  10.7 0.0 copy-done.6
  10.7 0.1 reshape.22.taps_in
  10.8 0.1 pad_add_fusion.place
  10.9 0.0 copy-done
  10.9 0.0 copy-done.1
  10.9 0.0 copy-done.2
  10.9 0.0 copy-done.3
  10.9 1.4 %project.1.part = f32[32,256]{1,0:T(8,128)S(1)} custom-call(s32[3]{0:T(128)S(1)} %pad_add_fusion.place, s32[1]{0:T(128)S(6)} %copy.12.count_in.count, f32[1,4]{1,0:T(1,128)S(1)} %copy-done.4, s32[1,4]{1,0:T(1,128)S(1)} %copy-done.5, f32[54]{0:T(128)S(1)} %reshape.22.taps_in, bf16[1536,128]{1,0:T(8,128)(2,1)S(1)} %bitcast.11, ...), custom_call_target="tpu_custom_call" | custom-call | flops 10000000000 | bytes 10000000 | tf_op jit(solution)/shard_map/project/pallas_call | solution.py:275
  12.4 0.0 collective-permute-done.partner
  12.4 0.6 %send.1 = bf16[16,24,128]{2,1,0:T(8,128)(2,1)S(1)} custom-call(s32[3]{0:T(128)S(1)} %pad_add_fusion.place, f32[32,256]{1,0:T(8,128)S(1)} %project.1.part, f32[8,128]{1,0:T(8,128)S(1)} %collective-permute-done.partner), custom_call_target="tpu_custom_call" | custom-call | tf_op jit(solution)/shard_map/send/pallas_call | solution.py:293
  13.0 21.4 %all_to_all.10 = bf16[16,24,128]{2,1,0:T(8,128)(2,1)S(1)} all-to-all(bf16[16,24,128]{2,1,0:T(8,128)(2,1)S(1)} %send.1), channel_id=1, replica_groups=mesh['snap'=16,'z'=16,'core'=2] {'z'}, dimensions={0} | all-to-all | bytes 196608 | tf_op jit(solution)/shard_map/all_to_all | solution.py:296
  34.3 0.6 %merge.1 = bf16[32,24,128]{2,1,0:T(8,128)(2,1)S(1)} custom-call(s32[3]{0:T(128)S(1)} %pad_add_fusion.place, bf16[384,128]{1,0:T(8,128)(2,1)S(1)} %bitcast.9), custom_call_target="tpu_custom_call" | custom-call | tf_op jit(solution)/shard_map/merge/pallas_call | solution.py:297
  35.0 16.9 %all_to_all.11 = bf16[32,24,128]{2,1,0:T(8,128)(2,1)S(1)} all-to-all(bf16[32,24,128]{2,1,0:T(8,128)(2,1)S(1)} %merge.1), channel_id=1, replica_groups=mesh['snap'=16,'z'=16,'core'=2] {'snap','core'}, dimensions={0} | all-to-all | bytes 393216 | tf_op jit(solution)/shard_map/all_to_all | solution.py:304
  51.9 1.9 %finish.1 = (f32[2,1,2,256]{3,2,1,0:T(2,128)}, f32[256,256]{1,0:T(8,128)}) custom-call(s32[3]{0:T(128)S(1)} %pad_add_fusion.place, bf16[768,128]{1,0:T(8,128)(2,1)S(1)} %bitcast.8), custom_call_target="tpu_custom_call" | custom-call | tf_op jit(solution)/shard_map/finish/pallas_call | solution.py:305
  (2 shorter events, 0.0 us)
Async XLA Ops:
  0.6 0.7 %copy-start.5 = (s32[1,4]{1,0:T(1,128)S(1)}, s32[1,4]{1,0:T(1,128)}, u32[]{:S(2)}) copy-start(s32[1,4]{1,0:T(1,128)} %blocks.3) | copy-start | bytes 52
  0.6 0.7 %copy-start.4 = (f32[1,4]{1,0:T(1,128)S(1)}, f32[1,4]{1,0:T(1,128)}, u32[]{:S(2)}) copy-start(f32[1,4]{1,0:T(1,128)} %spans.3) | copy-start | bytes 52
  1.3 9.4 %copy-start.6 = (f32[3,2,3,3]{3,1,2,0:T(2,128)S(1)}, f32[3,2,3,3]{3,1,2,0:T(2,128)}, u32[]{:S(2)}) copy-start(f32[3,2,3,3]{3,1,2,0:T(2,128)} %param.11) | copy-start | bytes 652
  1.3 9.6 %copy-start = (bf16[8,9,32,256]{3,2,1,0:T(8,128)(2,1)S(1)}, bf16[8,9,32,256]{3,2,1,0:T(8,128)(2,1)}, u32[]{:S(2)}) copy-start(bf16[8,9,32,256]{3,2,1,0:T(8,128)(2,1)} %param.13) | copy-start | bytes 3538948
  1.4 9.6 %copy-start.1 = (bf16[1,4,3,128,128]{4,3,2,1,0:T(8,128)(2,1)S(1)}, bf16[1,4,3,128,128]{4,3,2,1,0:T(8,128)(2,1)}, u32[]{:S(2)}) copy-start(bf16[1,4,3,128,128]{4,3,2,1,0:T(8,128)(2,1)} %param.8) | copy-start | bytes 1179652
  1.4 9.6 %copy-start.2 = (bf16[32,256]{1,0:T(8,128)(2,1)S(1)}, bf16[32,256]{1,0:T(8,128)(2,1)}, u32[]{:S(2)}) copy-start(bf16[32,256]{1,0:T(8,128)(2,1)} %stream.1) | copy-start | bytes 49156
  1.4 9.5 %copy-start.3 = (bf16[1,2,4,128]{3,2,1,0:T(4,128)(2,1)S(1)}, bf16[1,2,4,128]{3,2,1,0:T(4,128)(2,1)}, u32[]{:S(2)}) copy-start(bf16[1,2,4,128]{3,2,1,0:T(4,128)(2,1)} %param.15) | copy-start | bytes 6148
  2.0 10.4 %collective-permute-start = (f32[8,128]{1,0:T(8,128)S(1)}, f32[8,128]{1,0:T(8,128)S(1)}, u32[]{:S(2)}, u32[]{:S(2)}) collective-permute-start(f32[8,128]{1,0:T(8,128)S(1)} %pack.1), channel_id=1, source_target_pairs={{0,1},{1,0},{2,3},{3,2},{4,5},{5,4},{6,7},{7,6},{8,9},{9,8},{10,11... | collective-permute-start | bytes 12296 | tf_op jit(solution)/shard_map/ppermute | solution.py:274

commit v4 on v3

--- a/solution.py
+++ b/solution.py
@@ -13,7 +13,6 @@
 SMALL = 1.0 / 16.0
 LONG = pl.CostEstimate(flops=10**10, bytes_accessed=10**7, transcendentals=0)
 GRANT = pltpu.CompilerParams(vmem_limit_bytes=8 << 20)
-SMEM = pl.BlockSpec(memory_space=pltpu.SMEM)
 VMEM = pl.BlockSpec(memory_space=pltpu.VMEM)
 OVER_ROWS = (((0,), (0,)), ((), ()))
 
@@ -50,29 +49,31 @@
 
 
 def pack_kernel(count, spans, blocks, base, out):
-    last = count[0] - 1
     row = iota((8, 128), 0)
-    tile = jnp.where(row == 0, spans[0, 0], base[...])
-    tile = jnp.where(row == 1, blocks[0, 0].astype(jnp.float32), tile)
-    tile = jnp.where(row == 2, spans[0, last], tile)
-    out[...] = jnp.where(row == 3, blocks[0, last].astype(jnp.float32), tile)
-
-
-def project_kernel(place, count_in, spans, blocks, taps_in, vel, table, stream, shear, out, pooled):
-    count = count_in[0]
-    odd = place[0] == 1
+    last = iota((1, CAP), 1) == count[:, 0:CAP] - 1
+    marks = blocks[...].astype(jnp.float32)
+    tile = base[...]
+    for at, values in ((0, spans[...]), (1, marks)):
+        final = jnp.sum(jnp.where(last, values, 0.0), axis=1, keepdims=True)
+        tile = jnp.where(row == at, jnp.broadcast_to(values[:, 0:1], (8, 128)), tile)
+        tile = jnp.where(row == at + 2, jnp.broadcast_to(final, (8, 128)), tile)
+    out[...] = tile
+
+
+def project_kernel(
+    place, count_vec, spans_vec, blocks_vec, taps_vec, vel, table, stream, shear, out, pooled, count_in, spans, blocks, taps_in, sems
+):
+    pairs = ((taps_vec, taps_in), (count_vec, count_in), (spans_vec, spans), (blocks_vec, blocks))
+    copies = [pltpu.make_async_copy(source, target, sems.at[at]) for at, (source, target) in enumerate(pairs)]
+    for copy in copies:
+        copy.start()
+    odd = jnp.broadcast_to(place[0:1, 0:1], (96, 256)) == 1
 
     lane = iota((128, 128), 1)
     gap = iota((128, 128), 0) - 4 * (lane % 32) - lane // 32 + 1
     pool = jnp.where((gap >= 0) & (gap < 4) & (lane < 96), 1.0, 0.0).astype(jnp.bfloat16)
     group = iota((8, 128), 1) // 32
 
-    def tap(i, q, a):
-        at = ((i * 2 + q) * 3 + a) * 3
-        picked = jnp.where(group == 0, taps_in[at], jnp.where(group == 1, taps_in[at + 1], taps_in[at + 2]))
-        return jnp.where(group < 3, picked * SMALL, 0.0)
-
-    taps = {(i, q, a): tap(i, q, a) for i in range(3) for q in range(2) for a in range(3)}
     zeros = jnp.zeros((32, 256), jnp.bfloat16)
     omega = stream[...]
     spread = jnp.concatenate([omega, zeros, zeros, zeros], axis=0)
@@ -83,6 +84,16 @@
     planes, normals = [], []
     for c in range(CAP):
         pooled[pl.ds(PAD + c * 384, 384), :] = dot(vel[pl.ds(c * 384, 384), :], pool)
+    for copy in copies:
+        copy.wait()
+    count = count_in[0, 0]
+
+    def tap(i, q, a):
+        at = ((i * 2 + q) * 3 + a) * 3
+        picked = jnp.where(group == 0, taps_in[at], jnp.where(group == 1, taps_in[at + 1], taps_in[at + 2]))
+        return jnp.where(group < 3, picked * SMALL, 0.0)
+
+    taps = {(i, q, a): tap(i, q, a) for i in range(3) for q in range(2) for a in range(3)}
     for c in range(CAP):
         feats, centres = [], []
         for i in range(3):
@@ -149,7 +160,7 @@
 
 
 def send_kernel(place, part, partner, out):
-    odd = place[0] == 1
+    odd = jnp.broadcast_to(place[0:1, :], (8, 128)) == 1
     tile = partner[...]
     row = iota((8, 128), 0)
 
@@ -183,7 +194,7 @@
 
 
 def merge_kernel(place, rows, out, wide):
-    odd = place[0] == 1
+    odd = jnp.broadcast_to(place[0:1, :], (16, 128)) == 1
     chips = rows.shape[0] // SENT
     wide[...] = rows[...].astype(jnp.float32)
 
@@ -220,7 +231,7 @@
         out[copy_at] = whole
 
 
-def finish_kernel(place, rows, sketch, gram, wide, full):
+def finish_kernel(place, rows, sketch, gram, wide):
     wide[...] = rows[...].astype(jnp.float32)
 
     def across(at):
@@ -249,39 +260,50 @@
         OVER_ROWS,
         preferred_element_type=jnp.float32,
     )
-    core, chip, snap = place[0], place[1], place[2]
-    at = SENT * core + chip // 2
-    mine_high = across(at).astype(jnp.bfloat16)
-    mine_low = across(at + 8).astype(jnp.bfloat16)
-    mine = jnp.concatenate([mine_high, mine_high, mine_low], axis=0)
-    full[...] = lax.dot_general(mine, left, OVER_ROWS, preferred_element_type=jnp.float32)
-    base = (chip % 2) * 64 + 2 * snap
+    core, chip, snap = (jnp.broadcast_to(place[at : at + 1, :], (16, 128)) for at in range(3))
+    row_at = core * 8 + lax.shift_right_logical(chip, 1)
+    mine = jnp.zeros((16, 128), jnp.float32)
+    for c in range(2):
+        for r in range(8):
+            at = SENT * c + r
+            mine = jnp.where(row_at == c * 8 + r, across(at) + across(at + 8), mine)
+    target = iota((16, 128), 1) - (chip & 1) * 64 - 2 * snap
     for m in range(2):
         for x in range(2):
-            sketch[m, 0, x : x + 1, :] = full[pl.ds(base + 32 * m + x, 1), :]
+            column = jnp.sum(jnp.where(target == 32 * m + x, mine, 0.0), axis=1, keepdims=True)
+            sketch[m, 0, x : x + 1, :] = jnp.sum(column * coef, axis=0, keepdims=True)
 
 
 def per_device(velocity, plane_count, inv_span, kernels, omega_block, omega_table, omega_stream, wall_shear):
     f32, bf16 = jnp.float32, jnp.bfloat16
     chips, snaps = lax.axis_size("z"), lax.axis_size("snap")
     snap, z, core = lax.axis_index("snap"), lax.axis_index("z"), lax.axis_index("core")
-    place = jnp.stack([core, z, snap]).astype(jnp.int32)
+    row = iota((8, 128), 0)
+    place = jnp.where(row == 0, core, jnp.where(row == 1, z, snap)).astype(jnp.int32)
+    count = jnp.broadcast_to(plane_count.reshape(1, 1), (1, 128))
     tile = jax.ShapeDtypeStruct((8, 128), f32)
     base = call(blank_kernel, "blank", tile, [], cost=LONG)()
-    own = call(pack_kernel, "pack", tile, [SMEM, SMEM, SMEM, VMEM], cost=LONG)(
-        plane_count, inv_span, omega_block, base
+    own = call(pack_kernel, "pack", tile, [VMEM] * 4, cost=LONG)(
+        count, inv_span, omega_block, base
     )
     partner = lax.ppermute(own, "core", [(0, 1), (1, 0)])
     part = call(
         project_kernel,
         "project",
         jax.ShapeDtypeStruct((32, 256), f32),
-        [SMEM] * 5 + [VMEM] * 4,
-        [pltpu.VMEM((ROWS + 2 * PAD, 128), f32)],
+        [VMEM] * 9,
+        [
+            pltpu.VMEM((ROWS + 2 * PAD, 128), f32),
+            pltpu.SMEM((1, 128), jnp.int32),
+            pltpu.SMEM((1, CAP), f32),
+            pltpu.SMEM((1, CAP), jnp.int32),
+            pltpu.SMEM((54,), f32),
+            pltpu.SemaphoreType.DMA((4,)),
+        ],
         cost=LONG,
     )(
         place,
-        plane_count,
+        count,
         inv_span,
         omega_block,
         kernels.reshape(-1),
@@ -290,7 +312,7 @@
         omega_stream,
         wall_shear.reshape(8, 128),
     )
-    sent = call(send_kernel, "send", jax.ShapeDtypeStruct((chips, SENT, 128), bf16), [SMEM, VMEM, VMEM])(
+    sent = call(send_kernel, "send", jax.ShapeDtypeStruct((chips, SENT, 128), bf16), [VMEM] * 3)(
         place, part, partner
     )
     got = lax.all_to_all(sent, "z", 0, 0, tiled=True).reshape(chips * SENT, 128)
@@ -298,7 +320,7 @@
         merge_kernel,
         "merge",
         jax.ShapeDtypeStruct((snaps * 2, SENT, 128), bf16),
-        [SMEM, VMEM],
+        [VMEM, VMEM],
         [pltpu.VMEM((chips * SENT, 128), f32)],
     )(place, got)
     got = lax.all_to_all(sent, ("snap", "core"), 0, 0, tiled=True).reshape(snaps * 2 * SENT, 128)
@@ -306,8 +328,8 @@
         finish_kernel,
         "finish",
         (jax.ShapeDtypeStruct((2, 1, 2, 256), f32), jax.ShapeDtypeStruct((256, 256), f32)),
-        [SMEM, VMEM],
-        [pltpu.VMEM((snaps * 2 * SENT, 128), f32), pltpu.VMEM((128, 256), f32)],
+        [VMEM, VMEM],
+        [pltpu.VMEM((snaps * 2 * SENT, 128), f32)],
     )(place, got)
 
 

time: 54 us -> 51.9 us (0.961)
  Pallas kernels: 5.13 us -> 3.01 us
    pallas_call x1, Pallas kernels: 1.89 us -> 1.34 us  [per_device(): call(finish_kernel, 'finish', (jax.ShapeDtypeStruct((2, 1, 2, 256), f32),...]
    pallas_call x1, Pallas kernels: 0.62 us -> 0.08 us  [per_device(): call(send_kernel, 'send', jax.ShapeDtypeStruct((chips, SENT, 128), bf16),...]
    pallas_call x1, Pallas kernels: 0.64 us -> 0.1 us  [per_device(): call(merge_kernel, 'merge', jax.ShapeDtypeStruct((snaps * 2, SENT, 128),...]
where the time goes in v4:
time: 51.9 us; the launch traced here: 51.7 us
  blocking collectives  38.1 us (73%)
  starting transfers between devices  8.89 us (17%)
  Pallas kernels  3.01 us (6%)
  between operations  1.46 us (3%)
    all_to_all x1, blocking collectives, per_device(): got = lax.all_to_all(sent, 'z', 0, 0, tiled=True).reshape(chips * SENT, 128)  21.4 us
    all_to_all x1, blocking collectives, per_device(): lax.all_to_all(sent, ('snap', 'core'), 0, 0, tiled=True)  16.8 us
    ppermute x1, starting transfers between devices, per_device(): partner = lax.ppermute(own, 'core', [(0, 1), (1, 0)])  8.89 us
    pallas_call x1, Pallas kernels, per_device(): call(project_kernel, 'project', jax.ShapeDtypeStruct((32, 256), f32), [VM...  1.41 us
    pallas_call x1, Pallas kernels, per_device(): call(finish_kernel, 'finish', (jax.ShapeDtypeStruct((2, 1, 2, 256), f32),...  1.34 us
  transfers between devices with their start and end apart: 1, of which 0 were waited for; matrix products, arithmetic and copies ran while one was open for 0% of the time, Pallas kernels for 3%

profile of v4, /device:TPU:1, one launch (start us, length us, event | category | flops | bytes accessed | tf_op | source)
XLA Modules:
  0.0 51.7 jit_solution(12257443069764178455)
XLA Ops:
  0.6 0.0 copy-start.5
  0.6 0.0 copy-start.4
  1.3 0.0 copy-done.5
  1.3 0.0 copy-done.4
  1.3 0.0 copy-start.6
  1.4 0.0 copy-start
  1.4 0.0 copy-start.1
  1.4 0.0 copy-start.2
  1.4 0.0 copy-start.3
  1.4 0.1 pack.1
  1.5 8.9 %collective-permute-start = (f32[8,128]{1,0:T(8,128)S(1)}, f32[8,128]{1,0:T(8,128)S(1)}, u32[]{:S(2)}, u32[]{:S(2)}) collective-permute-start(f32[8,128]{1,0:T(8,128)S(1)} %pack.1), channel_id=1, source_target_pairs={{0,1},{1,0},{2,3},{3,2},{4,5},{5,4},{6,7},{7,6},{8,9},{9,8},{10,11... | collective-permute-start | bytes 12296 | tf_op jit(solution)/shard_map/ppermute | solution.py:289
  10.4 0.0 copy-done.6
  10.4 0.1 reshape.26.taps_vec
  10.5 0.1 broadcast_select_fusion.place
  10.6 0.0 copy-done
  10.6 0.0 copy-done.1
  10.6 0.0 copy-done.2
  10.6 0.0 copy-done.3
  10.6 1.4 %project.1.part = f32[32,256]{1,0:T(8,128)S(1)} custom-call(s32[8,128]{1,0:T(8,128)S(1)} %broadcast_select_fusion.place, s32[1,128]{1,0:T(1,128)S(1)} %broadcast_in_dim.23.count_vec.count, f32[1,4]{1,0:T(1,128)S(1)} %copy-done.4, s32[1,4]{1,0:T(1,128)S(1)} %copy-done.5, f32[54]{0:T(128)S(1)} %reshape.26.taps_vec, bf16[1536,128]{1,0:T(8,128)(2,1)S(1)} %bitcast.10, ...), custom_call_target="tpu_custom_call" | custom-call | flops 10000000000 | bytes 10000000 | tf_op jit(solution)/shard_map/project/pallas_call | solution.py:290
  12.0 0.0 collective-permute-done.partner
  12.1 0.1 send.1
  12.1 21.4 %all_to_all.10 = bf16[16,24,128]{2,1,0:T(8,128)(2,1)S(1)} all-to-all(bf16[16,24,128]{2,1,0:T(8,128)(2,1)S(1)} %send.1), channel_id=1, replica_groups=mesh['snap'=16,'z'=16,'core'=2] {'z'}, dimensions={0} | all-to-all | bytes 196608 | tf_op jit(solution)/shard_map/all_to_all | solution.py:318
  33.5 0.1 merge.1
  33.6 16.8 %all_to_all.11 = bf16[32,24,128]{2,1,0:T(8,128)(2,1)S(1)} all-to-all(bf16[32,24,128]{2,1,0:T(8,128)(2,1)S(1)} %merge.1), channel_id=1, replica_groups=mesh['snap'=16,'z'=16,'core'=2] {'snap','core'}, dimensions={0} | all-to-all | bytes 393216 | tf_op jit(solution)/shard_map/all_to_all | solution.py:326
  50.4 1.3 %finish.1 = (f32[2,1,2,256]{3,2,1,0:T(2,128)}, f32[256,256]{1,0:T(8,128)}) custom-call(s32[8,128]{1,0:T(8,128)S(1)} %broadcast_select_fusion.place, bf16[768,128]{1,0:T(8,128)(2,1)S(1)} %bitcast.7), custom_call_target="tpu_custom_call" | custom-call | tf_op jit(solution)/shard_map/finish/pallas_call | solution.py:327
  (5 shorter events, 0.0 us)
Async XLA Ops:
  0.6 0.7 %copy-start.5 = (s32[1,4]{1,0:T(1,128)S(1)}, s32[1,4]{1,0:T(1,128)}, u32[]{:S(2)}) copy-start(s32[1,4]{1,0:T(1,128)} %blocks.1) | copy-start | bytes 52
  0.6 0.7 %copy-start.4 = (f32[1,4]{1,0:T(1,128)S(1)}, f32[1,4]{1,0:T(1,128)}, u32[]{:S(2)}) copy-start(f32[1,4]{1,0:T(1,128)} %spans.1) | copy-start | bytes 52
  1.3 9.1 %copy-start.6 = (f32[3,2,3,3]{3,1,2,0:T(2,128)S(1)}, f32[3,2,3,3]{3,1,2,0:T(2,128)}, u32[]{:S(2)}) copy-start(f32[3,2,3,3]{3,1,2,0:T(2,128)} %param.11) | copy-start | bytes 652
  1.4 9.3 %copy-start = (bf16[8,9,32,256]{3,2,1,0:T(8,128)(2,1)S(1)}, bf16[8,9,32,256]{3,2,1,0:T(8,128)(2,1)}, u32[]{:S(2)}) copy-start(bf16[8,9,32,256]{3,2,1,0:T(8,128)(2,1)} %param.13) | copy-start | bytes 3538948
  1.4 9.2 %copy-start.1 = (bf16[1,4,3,128,128]{4,3,2,1,0:T(8,128)(2,1)S(1)}, bf16[1,4,3,128,128]{4,3,2,1,0:T(8,128)(2,1)}, u32[]{:S(2)}) copy-start(bf16[1,4,3,128,128]{4,3,2,1,0:T(8,128)(2,1)} %param.8) | copy-start | bytes 1179652
  1.4 9.2 %copy-start.2 = (bf16[32,256]{1,0:T(8,128)(2,1)S(1)}, bf16[32,256]{1,0:T(8,128)(2,1)}, u32[]{:S(2)}) copy-start(bf16[32,256]{1,0:T(8,128)(2,1)} %stream.1) | copy-start | bytes 49156
  1.4 9.2 %copy-start.3 = (bf16[1,2,4,128]{3,2,1,0:T(4,128)(2,1)S(1)}, bf16[1,2,4,128]{3,2,1,0:T(4,128)(2,1)}, u32[]{:S(2)}) copy-start(bf16[1,2,4,128]{3,2,1,0:T(4,128)(2,1)} %param.15) | copy-start | bytes 6148
  1.5 10.6 %collective-permute-start = (f32[8,128]{1,0:T(8,128)S(1)}, f32[8,128]{1,0:T(8,128)S(1)}, u32[]{:S(2)}, u32[]{:S(2)}) collective-permute-start(f32[8,128]{1,0:T(8,128)S(1)} %pack.1), channel_id=1, source_target_pairs={{0,1},{1,0},{2,3},{3,2},{4,5},{5,4},{6,7},{7,6},{8,9},{9,8},{10,11... | collective-permute-start | bytes 12296 | tf_op jit(solution)/shard_map/ppermute | solution.py:289
